TPU v7x, 256 devices: a whole 4x4x8 slice. The times are simulated.
256 devices in a mesh: dp: 8 (over y, x_hi), ctx: 32 (over x_lo, z, core).
Axes of the slice: x: 4 (x_hi: 2, x_lo: 2; x = x_hi * 2 + x_lo), y: 4, z: 8, core: 2. Of those that a mesh axis runs over, the one named last changes fastest.
Arguments:
- query_rows: bfloat16 [8, 4096, 2048], P('dp', 'ctx'), may hold values from -6 to 6
- key_rows: bfloat16 [8, 4096, 2048], P('dp', 'ctx'), may hold values from -6 to 6
- value_rows: bfloat16 [8, 4096, 2048], P('dp', 'ctx'), may hold values from -6 to 6
- norm_gain: float32 [2048], replicated, may hold values from 0.1 to 1.9
- out_weight: bfloat16 [2048, 2048], P('ctx'), may hold values from -0.125 to 0.125
- cotangent: bfloat16 [8, 4096, 2048], P('dp', 'ctx'), may hold values from -6 to 6
Outputs:
- mixed: bfloat16 [8, 4096, 2048], P('dp', 'ctx')
- grad_queries: bfloat16 [8, 4096, 2048], P('dp', 'ctx')
- grad_keys: bfloat16 [8, 4096, 2048], P('dp', 'ctx')
- grad_values: bfloat16 [8, 4096, 2048], P('dp', 'ctx')
- grad_weight: float32 [2048, 2048], P('ctx')
All inputs are finite; a program needn't handle non-finite values.
Results may differ from a plain program's by a relative error of at most 0.025.
Values may be sent and summed in bfloat16 or wider, within the bound.
A program may use at most 192 MiB of HBM per device.

v0:
```python
import math

import jax
import jax.numpy as jnp
from jax import lax
from jax.sharding import PartitionSpec as P

HEAD = 128


epsilon = 1e-06
highest_precision = lax.Precision.HIGHEST


def carried_in(value, axis, combine, identity):
    size, index = (lax.axis_size(axis), lax.axis_index(axis))
    everything = lax.all_gather(value, axis)
    start = jnp.broadcast_to(jnp.asarray(identity, value.dtype), value.shape)

    def carried_turn(k, before):
        reached = k < index
        new = combine(before, everything[k])
        return jnp.where(reached, new, before)

    return lax.fori_loop(0, size, carried_turn, start)


def entering(value, axis, combine, identity):
    size, index = (lax.axis_size(axis), lax.axis_index(axis))
    everything = lax.all_gather(value.astype(jnp.bfloat16), axis)
    start = jnp.broadcast_to(jnp.asarray(identity, value.dtype), value.shape)

    def entering_turn(k, before):
        at = size - 1 - k
        reached = at > index
        new = combine(before, everything[at].astype(value.dtype))
        return jnp.where(reached, new, before)

    return lax.fori_loop(0, size, entering_turn, start)


def feature(values):
    wide = values.astype(jnp.float32)
    return jnp.where(wide > 0, wide + 1.0, jnp.exp(jnp.minimum(wide, 0.0))).astype(jnp.bfloat16)


def feature_slope(values):
    wide = values.astype(jnp.float32)
    return jnp.where(wide > 0, 1.0, jnp.exp(jnp.minimum(wide, 0.0)))


def add_states(earlier, later):
    return earlier + later


def on_device(query_rows, key_rows, value_rows, norm_gain, out_weight, cotangent):
    length = query_rows.shape[1]
    width = query_rows.shape[2]
    heads = width // HEAD
    shape3 = (length, heads, HEAD)
    weight = lax.all_gather(out_weight, "ctx", axis=0, tiled=True)
    query_seq = query_rows[0]
    key_seq = key_rows[0]
    query_per_head = feature(query_seq).reshape(shape3)
    key_per_head = feature(key_seq).reshape(shape3)
    value_per_head = value_rows[0].reshape(shape3)
    local_state = jnp.einsum(
        "wmx,wmt->mxt", key_per_head, value_per_head, preferred_element_type=jnp.float32
    )
    zero_state = jnp.zeros_like(local_state)
    prefix_state = carried_in(local_state, "ctx", add_states, zero_state)
    causal = jnp.tril(jnp.ones((length, length), dtype=bool))
    scores = jnp.einsum(
        "thd,shd->hts", query_per_head, key_per_head, preferred_element_type=jnp.float32
    )
    probs = jnp.where(causal, scores, 0.0).astype(jnp.bfloat16)
    query_wide_rows = query_per_head.astype(jnp.float32)
    attended_output = jnp.einsum(
        "hts,shv->thv", probs, value_per_head, preferred_element_type=jnp.float32
    )
    attended_output = attended_output + jnp.einsum(
        "wrf,rfp->wrp", query_wide_rows, prefix_state, precision=highest_precision
    )
    inverse = lax.rsqrt(
        jnp.mean(attended_output * attended_output, axis=-1, keepdims=True) + epsilon
    )
    gain_heads = norm_gain.reshape(heads, HEAD)
    normed = (attended_output * inverse * gain_heads).reshape(length, width).astype(jnp.bfloat16)
    mixed = jnp.dot(normed, weight, preferred_element_type=jnp.float32).astype(jnp.bfloat16)
    upstream = cotangent[0]
    d_normed = lax.dot_general(
        upstream, weight, (((1,), (1,)), ((), ())), preferred_element_type=jnp.float32
    ).reshape(shape3)
    scaled = d_normed * gain_heads
    attended_gradient = (
        inverse
        * (
            scaled
            - attended_output
            * inverse
            * inverse
            * jnp.mean(scaled * attended_output, axis=-1, keepdims=True)
        )
    ).astype(jnp.bfloat16)
    grad_local = jnp.einsum(
        "ibg,ibq->bgq", query_per_head, attended_gradient, preferred_element_type=jnp.float32
    )
    suffix_state = entering(grad_local, "ctx", add_states, zero_state)
    d_scores = jnp.einsum(
        "thv,shv->hts", attended_gradient, value_per_head, preferred_element_type=jnp.float32
    )
    d_probs = jnp.where(causal, d_scores, 0.0).astype(jnp.bfloat16)
    wide_gradient = attended_gradient.astype(jnp.float32)
    value_wide_rows = value_per_head.astype(jnp.float32)
    key_wide_rows = key_per_head.astype(jnp.float32)
    query_gradient = jnp.einsum(
        "hts,shk->thk", d_probs, key_per_head, preferred_element_type=jnp.float32
    )
    query_gradient = query_gradient + jnp.einsum(
        "fxn,xpn->fxp", wide_gradient, prefix_state, precision=highest_precision
    )
    key_gradient = jnp.einsum(
        "hts,thk->shk", d_probs, query_per_head, preferred_element_type=jnp.float32
    )
    key_gradient = key_gradient + jnp.einsum(
        "mcu,cxu->mcx", value_wide_rows, suffix_state, precision=highest_precision
    )
    value_gradient = jnp.einsum(
        "hts,thv->shv", probs, attended_gradient, preferred_element_type=jnp.float32
    )
    value_gradient = value_gradient + jnp.einsum(
        "inz,nzc->inc", key_wide_rows, suffix_state, precision=highest_precision
    )
    grad_queries = (query_gradient.reshape(length, width) * feature_slope(query_seq)).astype(
        jnp.bfloat16
    )
    grad_keys = (key_gradient.reshape(length, width) * feature_slope(key_seq)).astype(jnp.bfloat16)
    grad_values = value_gradient.reshape(length, width).astype(jnp.bfloat16)
    devices_dp = lax.axis_size("dp")
    devices_ctx = lax.axis_size("ctx")
    loss_scale = 1.0 / math.sqrt(devices_dp * devices_ctx * length)
    shares = lax.psum_scatter(
        lax.dot_general(
            normed, upstream, (((0,), (0,)), ((), ())), preferred_element_type=jnp.float32
        ).astype(jnp.bfloat16),
        "ctx",
        scatter_dimension=0,
        tiled=True,
    )
    summed = lax.psum(shares, "dp").astype(jnp.float32)
    grad_weight = summed * loss_scale
    return (mixed[None], grad_queries[None], grad_keys[None], grad_values[None], grad_weight)


def solution(mesh):
    return jax.shard_map(
        on_device,
        mesh=mesh,
        in_specs=(
            P("dp", "ctx", None),
            P("dp", "ctx", None),
            P("dp", "ctx", None),
            P(),
            P("ctx", None),
            P("dp", "ctx", None),
        ),
        out_specs=(
            P("dp", "ctx", None),
            P("dp", "ctx", None),
            P("dp", "ctx", None),
            P("dp", "ctx", None),
            P("ctx", None),
        ),
        check_vma=False,
    )
```

profile of v0, /device:TPU:1, one launch (start us, length us, event | category | flops | bytes accessed | tf_op | source)
XLA Modules:
  0.0 674.6 jit_solution(1039800989723553245)
XLA Ops:
  12.7 2.1 fusion.6
  17.4 183.0 %all-gather.8.cloned.1.call-done = f32[512,128,128]{2,1,0:T(8,128)} async-done(((f32[16,128,128]{2,1,0:T(8,128)}), f32[512,128,128]{2,1,0:T(8,128)}) %all-gather.8.cloned.1.call-update) | async-done | bytes 33554448 | tf_op jit(solution)/shard_map/all_gather | solution.py:17
  200.4 52.2 %while.30 = (s32[]{:T(128)}, f32[16,128,128]{2,1,0:T(8,128)S(1)}, s32[]{:T(128)}, f32[32,16,128,128]{3,2,1,0:T(8,128)}, s32[]{:T(128)}, /*index=5*/s32[]{:T(128)}) while((s32[]{:T(128)}, f32[16,128,128]{2,1,0:T(8,128)S(1)}, s32[]{:T(128)}, f32[32,16,128,128]{3,2,1,0:T(8,128)}, s32[]{:T(128)}, /*index=5*/s32[]{:T(128)}) %tuple.93), condition=%wide.region_1.2_spmd.clone, body=%wide.region_0.1_spmd.clone.sunk | while | flops 786436 | bytes 3145821 | solution.py:25
  213.4 1.7 add_select_fusion.4
  218.4 1.6 add_select_fusion.4
  229.7 1.6 add_select_fusion.4
  231.4 1.6 add_select_fusion.4
  234.7 1.6 add_select_fusion.4
  241.2 1.6 add_select_fusion.4
  246.1 1.6 add_select_fusion.4
  247.7 1.6 add_select_fusion.4
  251.0 1.6 add_select_fusion.4
  255.3 19.7 %all-gather.6.cloned.1.call-done = bf16[2048,2048]{1,0:T(8,128)(2,1)} async-done(((bf16[64,2048]{1,0:T(8,128)(2,1)}), bf16[2048,2048]{1,0:T(8,128)(2,1)}) %all-gather.6.cloned.1.call-update) | async-done | bytes 8388624 | tf_op jit(solution)/shard_map/all_gather | solution.py:61
  275.0 5.7 multiply_reduce_fusion
  281.9 5.6 convolution_convert_fusion
  287.6 124.8 %reduce-scatter.2.cloned.1.call-done = bf16[64,2048]{1,0:T(8,128)(2,1)} async-done(((bf16[2048,2048]{1,0:T(8,128)(2,1)}), bf16[64,2048]{1,0:T(8,128)(2,1)}) %reduce-scatter.2.cloned.1.call-update) | async-done | bytes 262160 | tf_op jit(solution)/shard_map/reduce_scatter | solution.py:142
  414.0 1.7 fusion.4
  415.7 1.7 fusion.27
  417.5 2.7 convolution_add_fusion.2
  421.7 2.5 fusion.29
  424.1 2.3 fusion.28
  426.5 2.1 fusion.10
  428.6 5.5 fusion
  434.0 65.0 %all-reduce.2.cloned.1.call-done = bf16[64,2048]{1,0:T(8,128)(2,1)} async-done(((bf16[64,2048]{1,0:T(8,128)(2,1)}), bf16[64,2048]{1,0:T(8,128)(2,1)}) %all-reduce.2.cloned.1.call-update) | async-done | bytes 262160 | tf_op jit(solution)/shard_map/psum | solution.py:150
  499.0 1.8 convert_multiply_fusion
  500.8 103.3 %all-gather.10.cloned.1.call-done = bf16[512,128,128]{2,1,0:T(8,128)(2,1)} async-done(((bf16[16,128,128]{2,1,0:T(8,128)(2,1)}), bf16[512,128,128]{2,1,0:T(8,128)(2,1)}) %all-gather.10.cloned.1.call-update) | async-done | bytes 16777232 | tf_op jit(solution)/shard_map/all_gather | solution.py:30
  604.1 52.7 %while.31 = (s32[]{:T(128)}, f32[16,128,128]{2,1,0:T(8,128)S(1)}, s32[]{:T(128)}, bf16[32,16,128,128]{3,2,1,0:T(8,128)(2,1)}, s32[]{:T(128)}, /*index=5*/s32[]{:T(128)}, s32[]{:T(128)}, s32[]{:T(128)}) while((s32[]{:T(128)}, f32[16,128,128]{2,1,0:T(8,128)S(1)}, s32[]{:T(128)}, bf16[32,16,128,128]{3,2,1,0:T(8,128)(2,1)}, s32[]{:T(128)}, ...), condition=%wide.region_5.6_spmd.clone, body=%wide.region_4.5_spmd.clone.sunk | while | flops 1048584 | bytes 2621595 | solution.py:39
  604.1 1.7 add_select_fusion.5
  605.8 1.6 add_select_fusion.5
  656.8 3.1 fusion.2
  659.9 2.0 copy.50
  662.0 3.4 convolution_add_fusion.1
  (109 shorter events, 102.8 us)
Async XLA Ops:
  7.2 267.8 %copy-start = (bf16[1,128,2048]{2,1,0:T(8,128)(2,1)S(1)}, bf16[1,128,2048]{2,1,0:T(8,128)(2,1)}, u32[]{:S(2)}) copy-start(bf16[1,128,2048]{2,1,0:T(8,128)(2,1)} %param.15) | copy-start | bytes 1572868
  7.2 193.3 %all-gather.8.cloned.1.call-start = ((), (), s32[]{:S(2)}) async-start(), calls=%async_computation.4 | async-start | bytes 34603008 | tf_op jit(solution)/shard_map/all_gather | solution.py:17
  8.7 191.7 %copy-start.8 = (bf16[16,8,16,128]{3,2,1,0:T(8,128)(2,1)}, bf16[16,8,16,128]{3,2,1,0:T(8,128)(2,1)S(1)}, u32[]{:S(2)}) copy-start(bf16[16,8,16,128]{3,2,1,0:T(8,128)(2,1)S(1)} %copy.57) | copy-start | bytes 1572868
  9.2 3.5 copy-start.10
  10.6 243.1 %copy-start.5 = (bf16[16,8,16,128]{3,2,1,0:T(8,128)(2,1)}, bf16[16,8,16,128]{3,2,1,0:T(8,128)(2,1)S(1)}, u32[]{:S(2)}) copy-start(bf16[16,8,16,128]{3,2,1,0:T(8,128)(2,1)S(1)} %copy.58) | copy-start | bytes 1572868
  11.9 263.1 %all-gather.6.cloned.1.call-start = ((), (), s32[]{:S(2)}) async-start(), calls=%async_computation.1 | async-start | bytes 8650752 | tf_op jit(solution)/shard_map/all_gather | solution.py:61
  12.6 399.8 %reduce-scatter.2.cloned.1.call-start = ((), (), s32[]{:S(2)}) async-start(), calls=%async_computation.2 | async-start | bytes 8650752 | tf_op jit(solution)/shard_map/reduce_scatter | solution.py:142
  16.1 236.6 %copy-start.2 = (bf16[1,128,2048]{1,2,0:T(8,128)(2,1)}, bf16[1,128,2048]{1,2,0:T(8,128)(2,1)S(1)}, u32[]{:S(2)}) copy-start(bf16[1,128,2048]{1,2,0:T(8,128)(2,1)S(1)} %copy.56) | copy-start | bytes 1572868
  200.4 74.6 %copy-start.13 = (f32[2048]{0:T(1024)S(1)}, f32[2048]{0:T(1024)}, u32[]{:S(2)}) copy-start(f32[2048]{0:T(1024)} %param.13) | copy-start | bytes 24580
  281.9 130.8 %copy-start.3 = (bf16[1,128,2048]{1,2,0:T(8,128)(2,1)S(1)}, bf16[1,128,2048]{1,2,0:T(8,128)(2,1)}, u32[]{:S(2)}) copy-start(bf16[1,128,2048]{1,2,0:T(8,128)(2,1)} %copy-done.2) | copy-start | bytes 1572868
  281.9 130.8 %copy-start.7 = (bf16[128,16,128]{0,2,1:T(8,128)(2,1)S(1)}, bf16[128,16,128]{0,2,1:T(8,128)(2,1)}, u32[]{:S(2)}) copy-start(bf16[128,16,128]{0,2,1:T(8,128)(2,1)} %get-tuple-element.254) | copy-start | bytes 1572868
  287.5 136.6 %copy-start.4 = (bf16[1,128,2048]{1,2,0:T(8,128)(2,1)S(1)}, bf16[1,128,2048]{1,2,0:T(8,128)(2,1)}, u32[]{:S(2)}) copy-start(bf16[1,128,2048]{1,2,0:T(8,128)(2,1)} %copy-done.2) | copy-start | bytes 1572868
  287.6 211.5 %all-reduce.2.cloned.1.call-start = ((), (), s32[]{:S(2)}) async-start(), calls=%async_computation.3 | async-start | bytes 524288 | tf_op jit(solution)/shard_map/psum | solution.py:150
  412.5 191.6 %all-gather.10.cloned.1.call-start = ((), (), s32[]{:S(2)}) async-start(), calls=%async_computation.5 | async-start | bytes 17301504 | tf_op jit(solution)/shard_map/all_gather | solution.py:30
  415.7 4.4 copy-start.12
  434.0 222.8 %copy-start.9 = (bf16[16,8,16,128]{3,2,1,0:T(8,128)(2,1)S(1)}, bf16[16,8,16,128]{3,2,1,0:T(8,128)(2,1)}, u32[]{:S(2)}) copy-start(bf16[16,8,16,128]{3,2,1,0:T(8,128)(2,1)} %copy-done.8) | copy-start | bytes 1572868
  604.1 57.9 %copy-start.6 = (bf16[16,8,16,128]{3,2,1,0:T(8,128)(2,1)S(1)}, bf16[16,8,16,128]{3,2,1,0:T(8,128)(2,1)}, u32[]{:S(2)}) copy-start(bf16[16,8,16,128]{3,2,1,0:T(8,128)(2,1)} %copy-done.5) | copy-start | bytes 1572868
  604.1 62.9 %copy-start.11 = (bf16[1,128,2048]{2,1,0:T(8,128)(2,1)S(1)}, bf16[1,128,2048]{2,1,0:T(8,128)(2,1)}, u32[]{:S(2)}) copy-start(bf16[1,128,2048]{2,1,0:T(8,128)(2,1)} %param.11) | copy-start | bytes 1572868
  656.8 11.2 %copy-start.1 = (bf16[1,128,2048]{2,1,0:T(8,128)(2,1)S(1)}, bf16[1,128,2048]{2,1,0:T(8,128)(2,1)}, u32[]{:S(2)}) copy-start(bf16[1,128,2048]{2,1,0:T(8,128)(2,1)} %param.15) | copy-start | bytes 1572868
Sparse Core Ops, SparseCore 0:
  12.0 188.4 all-gather.7
  202.3 72.6 all-gather.5
  287.7 124.7 reduce-scatter.1
  414.9 84.0 all-reduce.1
  500.9 103.1 all-gather.9
where the time goes:
time: 678 us; the launch traced here: 675 us
  waiting for transfers between devices  497 us (73%)
  other arithmetic  113 us (17%)
  matrix products  40.6 us (6%)
  between operations  14 us (2%)
  local copies, waits for them, and re-layouts  8.44 us (1%)
    all_gather x1, waiting for transfers between devices, carried_in(): everything = lax.all_gather(value, axis)  183 us
    reduce_scatter x1, waiting for transfers between devices, on_device(): lax.psum_scatter(lax.dot_general(normed, upstream, (((0,), (0,)), ((), ()...  125 us
    all_gather x1, waiting for transfers between devices, entering(): everything = lax.all_gather(value.astype(jnp.bfloat16), axis)  103 us
    psum x1, waiting for transfers between devices, on_device(): summed = lax.psum(shares, 'dp').astype(jnp.float32)  65 us
    select_n x32, other arithmetic, entering_turn(): return jnp.where(reached, new, before)  51.8 us
    select_n x32, other arithmetic, carried_turn(): return jnp.where(reached, new, before)  51.4 us
    all_gather x1, waiting for transfers between devices, on_device(): weight = lax.all_gather(out_weight, 'ctx', axis=0, tiled=True)  19.7 us
  transfers between devices with their start and end apart: 5, of which 5 were waited for; matrix products, arithmetic and copies ran while one was open for 12% of the time, Pallas kernels for 0%

commit v1 on v0

v1 whole, which is shorter than its diff:
```python
import math

import jax
import jax.numpy as jnp
from jax import lax
from jax.experimental import pallas as pl
from jax.experimental.pallas import tpu as pltpu
from jax.sharding import PartitionSpec as P

MESH = pl.DeviceIdType.MESH
F32 = jnp.float32
BF16 = jnp.bfloat16
HEAD = 128
EPSILON = 1e-06
NZ = 8
NX = 4
NY = 4
CHIPS = 16
HALF = 1024


def dot(a, b, ca, cb):
    return lax.dot_general(a, b, (((ca,), (cb,)), ((), ())), preferred_element_type=F32)


def rcopy(src, dst, send, recv, device):
    return pltpu.make_async_remote_copy(
        src_ref=src, dst_ref=dst, send_sem=send, recv_sem=recv, device_id=device, device_id_type=MESH
    )


def exp_low(wide):
    return jnp.exp(jnp.minimum(wide, 0.0))


def feature(values):
    wide = values.astype(F32)
    return jnp.where(wide > 0, wide + 1.0, exp_low(wide)).astype(BF16)


def slope(values):
    wide = values.astype(F32)
    return jnp.where(wide > 0, 1.0, exp_low(wide))


def kernel(
    loss_scale,
    q_ref, k_ref, v_ref, gain_ref, w_ref, cot_ref,
    mixed_ref, gq_ref, gk_ref, gv_ref, gw_ref,
    fq, fk, probs, att, dnorm, normed, datt, dfk, dgv, local, state,
    xsend, xrecv, pieces, got, back_out, back_in, psend, prefix, suffix,
    wfull, cotg, normg, gwf, gwt, xh_in, x_out, x_in, z_out, z_in, f_out, f_in,
    sx_s, sx_r, s1_s, s1_r, s2_s, s2_r, sp_s, sp_r,
    up_s, up_r, dn_s, dn_r, wx_s, wx_r, wp_s, wp_r,
    cu_s, cu_r, cd_s, cd_r, cp_s, cp_r,
    n_s, n_r, xa_s, xa_r, xb_s, xb_r, z_s, z_r, f_s, f_r,
):
    d = lax.axis_index("dp")
    i = lax.axis_index("ctx")
    c = i % 2
    j = i // 2
    z = j % NZ
    xl = j // NZ
    y = d // 2
    xh = d % 2
    x = xh * 2 + xl
    o = 1 - c
    partner = (d, j * 2 + o)

    def chip(jj):
        return (d, jj * 2 + c)

    def at_x(xx):
        return (y * 2 + xx // 2, ((xx % 2) * NZ + z) * 2 + c)

    def at_z(zz):
        return (d, (xl * NZ + zz) * 2 + c)

    def at_y(yy, cc):
        return (yy * 2 + xh, j * 2 + cc)

    def final_to(t):
        return (t, 8 * y + 4 * c + x)

    from_x = i % 4
    from_c = (i // 4) % 2
    from_d = (i // 8) * 2 + from_x // 2

    def final_from(zz):
        return (from_d, ((from_x % 2) * NZ + zz) * 2 + from_c)

    def same(device):
        return jnp.logical_and(device[0] == d, device[1] == i)

    barrier = pltpu.get_barrier_semaphore()

    def greet(device):
        pl.semaphore_signal(barrier, inc=1, device_id=device, device_id_type=MESH)

    def greet_maybe_self(device):
        @pl.when(jnp.logical_not(same(device)))
        def _():
            greet(device)

    for t in range(1, CHIPS):
        greet(chip((j + t) % CHIPS))
    greet(partner)
    for t in range(1, NX):
        greet(at_x((x + t) % NX))
    for t in range(1, NY):
        greet(at_y((y + t) % NY, 0))
        greet(at_y((y + t) % NY, 1))
    for t in range(8):
        greet_maybe_self(final_to(t))
        greet_maybe_self(final_from(t))

    def head(h):
        return pl.ds(pl.multiple_of(h * HEAD, HEAD), HEAD)

    def loop_a(h, _):
        cols = head(h)
        fq[:, cols] = feature(q_ref[:, cols])
        kf = feature(k_ref[:, cols])
        fk[:, cols] = kf
        local[h] = dot(kf, v_ref[:, cols], 0, 0)
        return 0

    lax.fori_loop(0, 16, loop_a, 0, unroll=2)

    selves = jnp.where(8 * y + 4 * c + x == i, 2, 0)
    pl.semaphore_wait(barrier, 15 + 1 + 3 + 6 + 16 - selves)

    left = pl.ds(0, HALF)
    right = pl.ds(HALF, HALF)

    pending = []

    def begin(copy):
        copy.start()
        pending.append(copy)
        return copy

    def wslot(zz):
        return (xl * NZ + zz) * 2 + c

    def oslot(zz):
        return ((1 - xl) * NZ + zz) * 2 + c

    near_x = (y * 2 + xh, ((1 - xl) * NZ + z) * 2 + c)
    far_x = (y * 2 + (1 - xh), ((1 - xl) * NZ + z) * 2 + c)
    z_up = at_z((z + 1) % NZ)
    z_dn = at_z((z + NZ - 1) % NZ)

    def wsrc(r, cols=None):
        if r == 0:
            return w_ref if cols is None else w_ref.at[:, cols]
        slot = wslot((z + r) % NZ)
        return wfull.at[slot] if cols is None else wfull.at[slot, :, cols]

    def wdst(r, cols=None):
        slot = wslot((z + r) % NZ)
        return wfull.at[slot] if cols is None else wfull.at[slot, :, cols]

    def w_up(k):
        cols = left if k == 3 else None
        r = (-k) % NZ
        return rcopy(wsrc(r, cols), wdst(r, cols), up_s.at[k], up_r.at[k], z_up)

    def w_dn(k):
        cols = right if k == 3 else None
        return rcopy(wsrc(k, cols), wdst(k, cols), dn_s.at[k], dn_r.at[k], z_dn)

    def w_up_wait(k):
        r = (-k - 1) % NZ
        cols = left if k == 3 else None
        ref = wdst(r, cols)
        rcopy(ref, ref, up_s.at[k], up_r.at[k], z_up).wait_recv()

    def w_dn_wait(k):
        cols = right if k == 3 else None
        ref = wdst(k + 1, cols)
        rcopy(ref, ref, dn_s.at[k], dn_r.at[k], z_dn).wait_recv()

    def w_near(r):
        begin(rcopy(wsrc(r, left), wdst(r, left), wx_s.at[r, 0], wx_r.at[r, 0], near_x))

    def w_far(r):
        begin(rcopy(wsrc(r, right), wdst(r, right), wx_s.at[r, 1], wx_r.at[r, 1], far_x))

    def w_pair(r):
        begin(rcopy(wsrc(r), wdst(r), wp_s.at[r], wp_r.at[r], partner))

    def w_first():
        begin(w_up(0))
        begin(w_dn(0))
        w_near(0)
        w_far(0)
        w_pair(0)

    def w_step(k):
        w_up_wait(k - 1)
        begin(w_up(k))
        w_dn_wait(k - 1)
        begin(w_dn(k))
        for r in ((-k) % NZ, k):
            w_near(r)
            w_far(r)
            w_pair(r)

    def w_last():
        w_up_wait(3)
        w_near(4)
        w_dn_wait(3)
        w_far(4)
        w_pair(4)

    def w_other(r):
        slot = oslot((z + r) % NZ)
        for a, cols in ((0, left), (1, right)):
            ref = wfull.at[slot, :, cols]
            rcopy(ref, ref, wx_s.at[r, a], wx_r.at[r, a], near_x).wait_recv()
        begin(rcopy(wfull.at[slot], wfull.at[slot], wp_s.at[8 + r], wp_r.at[8 + r], partner))

    def w_pair_wait():
        for r in range(16):
            zz = (z + r) % NZ
            side = xl if r < 8 else 1 - xl
            ref = wfull.at[(side * NZ + zz) * 2 + o]
            rcopy(ref, ref, wp_s.at[r], wp_r.at[r], partner).wait_recv()

    y_up = at_y((y + 1) % NY, c)
    y_dn = at_y((y + NY - 1) % NY, c)

    def cslot(r):
        return ((y + r) % NY) * 2 + c

    def c_first():
        own = cotg.at[cslot(0)]
        begin(rcopy(cot_ref, own, cu_s.at[0], cu_r.at[0], y_up))
        begin(rcopy(cot_ref, own, cd_s.at[0], cd_r.at[0], y_dn))
        begin(rcopy(cot_ref, own, cp_s.at[0], cp_r.at[0], partner))

    def c_pair(r):
        ref = cotg.at[cslot(r)]
        begin(rcopy(ref, ref, cp_s.at[r], cp_r.at[r], partner))

    def c_second():
        below = cotg.at[cslot(3)]
        rcopy(below, below, cu_s.at[0], cu_r.at[0], y_up).wait_recv()
        part = cotg.at[cslot(3), :, left]
        begin(rcopy(part, part, cu_s.at[1], cu_r.at[1], y_up))
        above = cotg.at[cslot(1)]
        rcopy(above, above, cd_s.at[0], cd_r.at[0], y_dn).wait_recv()
        part = cotg.at[cslot(1), :, right]
        begin(rcopy(part, part, cd_s.at[1], cd_r.at[1], y_dn))
        c_pair(3)
        c_pair(1)

    def c_third():
        a = cotg.at[cslot(2), :, left]
        rcopy(a, a, cu_s.at[1], cu_r.at[1], y_up).wait_recv()
        b = cotg.at[cslot(2), :, right]
        rcopy(b, b, cd_s.at[1], cd_r.at[1], y_dn).wait_recv()
        c_pair(2)

    def c_wait():
        for r in range(4):
            ref = cotg.at[((y + r) % NY) * 2 + o]
            rcopy(ref, ref, cp_s.at[r], cp_r.at[r], partner).wait_recv()

    own_heads = pl.ds(8 * c, 8)
    other_heads = pl.ds(8 * o, 8)

    def scan_pair(n):
        xsend[n] = local[other_heads].astype(BF16)
        begin(rcopy(xsend.at[n], xrecv.at[n], sx_s.at[n], sx_r.at[n], partner))

    def scan_spread(n):
        rcopy(xrecv.at[n], xrecv.at[n], sx_s.at[n], sx_r.at[n], partner).wait_recv()
        total = (local[own_heads] + xrecv[n].astype(F32)).astype(BF16)
        pieces[n] = total.reshape(CHIPS, 64, HEAD)
        for t in range(1, CHIPS):
            jj = (j + t) % CHIPS
            begin(rcopy(pieces.at[n, jj], got.at[n, j], s1_s.at[n, jj], s1_r.at[n, j], chip(jj)))
        got[n, j] = pieces[n, j]

    def scan_return(n):
        for t in range(1, CHIPS):
            jj = (j + t) % CHIPS
            ref = got.at[n, jj]
            rcopy(ref, ref, s1_s.at[n, jj], s1_r.at[n, jj], partner).wait_recv()
        total = jnp.zeros((64, HEAD), F32)
        order = range(CHIPS) if n == 0 else range(CHIPS - 1, -1, -1)
        for jj in order:
            back_out[n, jj] = total.astype(BF16)
            total = total + got[n, jj].astype(F32)
        for t in range(1, CHIPS):
            jj = (j + t) % CHIPS
            begin(rcopy(back_out.at[n, jj], back_in.at[n, j], s2_s.at[n, jj], s2_r.at[n, j], chip(jj)))
        back_in[n, j] = back_out[n, j]

    def scan_share(n, out):
        for t in range(1, CHIPS):
            jj = (j + t) % CHIPS
            ref = back_in.at[n, jj]
            rcopy(ref, ref, s2_s.at[n, jj], s2_r.at[n, jj], partner).wait_recv()
        mine = back_in[n].astype(F32).reshape(8, HEAD, HEAD)
        last = (c if n == 0 else o).astype(F32)
        psend[n] = (mine + (1.0 - last) * local[own_heads]).astype(BF16)
        begin(rcopy(psend.at[n], out.at[own_heads], sp_s.at[n], sp_r.at[n], partner))
        out[own_heads] = (mine + last * xrecv[n].astype(F32)).astype(BF16)

    def scan_wait(n, out):
        ref = out.at[other_heads]
        rcopy(ref, ref, sp_s.at[n], sp_r.at[n], partner).wait_recv()

    scan_pair(0)
    w_first()
    c_first()
    scan_spread(0)

    rows_at = lax.broadcasted_iota(jnp.int32, (HEAD, HEAD), 0)
    cols_at = lax.broadcasted_iota(jnp.int32, (HEAD, HEAD), 1)
    causal = rows_at >= cols_at

    def loop_b(h, _):
        cols = head(h)
        scores = dot(fq[:, cols], fk[:, cols], 1, 1)
        p = jnp.where(causal, scores, 0.0).astype(BF16)
        probs[h] = p
        att[:, cols] = dot(p, v_ref[:, cols], 1, 0)
        return 0

    lax.fori_loop(0, 16, loop_b, 0, unroll=2)
    wfull[i] = w_ref[...]
    cotg[cslot(0)] = cot_ref[...]

    w_step(1)
    scan_return(0)
    w_other(0)
    w_step(2)
    c_second()
    scan_share(0, prefix)
    w_other(7)
    w_other(1)
    w_step(3)
    scan_wait(0, prefix)
    w_other(6)
    w_other(2)
    w_last()
    c_third()
    for r in (5, 3, 4):
        w_other(r)
    w_pair_wait()

    def loop_c(h2, _):
        cols = pl.ds(pl.multiple_of(h2 * 256, 256), 256)
        rows = wfull[pl.ds(h2 * 4, 4)].reshape(256, 2048)
        dnorm[:, cols] = dot(cot_ref[...], rows, 1, 1) * gain_ref[:, cols]
        return 0

    lax.fori_loop(0, 8, loop_c, 0)

    def loop_d(h, _):
        cols = head(h)
        fqh = fq[:, cols]
        a = att[:, cols] + dot(fqh, prefix[h], 1, 0)
        inverse = lax.rsqrt(jnp.mean(a * a, axis=-1, keepdims=True) + EPSILON)
        ai = a * inverse
        normed[:, cols] = (ai * gain_ref[:, cols]).astype(BF16)
        s = dnorm[:, cols]
        m = jnp.mean(s * a, axis=-1, keepdims=True)
        g = (inverse * (s - ai * inverse * m)).astype(BF16)
        datt[:, cols] = g
        local[h] = dot(fqh, g, 0, 0)
        return 0

    lax.fori_loop(0, 16, loop_d, 0, unroll=2)

    me8 = y * 2 + c

    def block8(b):
        return pl.ds(pl.multiple_of(b * 256, 256), 256)

    scan_pair(1)
    for t in range(1, 8):
        b = (me8 + t) % 8
        begin(
            rcopy(
                normed.at[:, block8(b)], normg.at[me8], n_s.at[b], n_r.at[me8], at_y(b // 2, b % 2)
            )
        )
    normg[me8] = normed[:, block8(me8)]
    scan_spread(1)

    def loop_e(h, _):
        cols = head(h)
        g = datt[:, cols]
        vh = v_ref[:, cols]
        fkh = fk[:, cols]
        fqh = fq[:, cols]
        dp = jnp.where(causal, dot(g, vh, 1, 1), 0.0).astype(BF16)
        dfq = dot(dp, fkh, 1, 0) + dot(g, prefix[h], 1, 1)
        gq_ref[:, cols] = (dfq * slope(q_ref[:, cols])).astype(BF16)
        dfk[:, cols] = dot(dp, fqh, 0, 0)
        dgv[:, cols] = dot(probs[h], g, 0, 0)
        return 0

    lax.fori_loop(0, 16, loop_e, 0, unroll=2)

    c_wait()
    for t in range(1, 8):
        b = (me8 + t) % 8
        ref = normg.at[b]
        rcopy(ref, ref, n_s.at[b], n_r.at[b], partner).wait_recv()

    def loop_g(n, _):
        cols = pl.ds(pl.multiple_of(n * 512, 512), 512)
        a = normg[...].reshape(1024, 256)
        b = cotg[:, :, cols].reshape(1024, 512)
        tile = dot(a, b, 0, 0)
        gwf[:, :, cols] = tile.reshape(4, 64, 512)
        gwt[:, :, cols] = tile.astype(BF16).reshape(4, 64, 512)
        return 0

    lax.fori_loop(0, 4, loop_g, 0)

    x_up = at_x((x + 1) % NX)
    x_dn = at_x((x + 3) % NX)
    two = (x + 2) % NX
    begin(rcopy(gwt.at[two, :, left], xh_in.at[0], xa_s.at[0], xa_r.at[0], x_up))
    begin(rcopy(gwt.at[two, :, right], xh_in.at[1], xa_s.at[1], xa_r.at[1], x_dn))
    scan_return(1)
    for a, to in ((0, x_up), (1, x_dn)):
        rcopy(xh_in.at[a], xh_in.at[a], xa_s.at[a], xa_r.at[a], to).wait_recv()
    one_up = (x + 1) % NX
    one_dn = (x + 3) % NX
    x_out[0, :, left] = (gwf[one_up, :, left] + xh_in[0].astype(F32)).astype(BF16)
    x_out[0, :, right] = gwt[one_up, :, right]
    x_out[1, :, left] = gwt[one_dn, :, left]
    x_out[1, :, right] = (gwf[one_dn, :, right] + xh_in[1].astype(F32)).astype(BF16)
    begin(rcopy(x_out.at[0], x_in.at[0], xb_s.at[0], xb_r.at[0], x_up))
    begin(rcopy(x_out.at[1], x_in.at[1], xb_s.at[1], xb_r.at[1], x_dn))

    def loop_m(n, _):
        cols = pl.ds(pl.multiple_of(n * 512, 512), 512)
        rows = wfull[:, :, cols].reshape(2048, 512)
        mixed_ref[:, cols] = dot(normed[...], rows, 1, 0).astype(BF16)
        return 0

    lax.fori_loop(0, 4, loop_m, 0)

    scan_share(1, suffix)
    for a, to in ((0, x_up), (1, x_dn)):
        rcopy(x_in.at[a], x_in.at[a], xb_s.at[a], xb_r.at[a], to).wait_recv()
    total = gwf[x] + x_in[0].astype(F32) + x_in[1].astype(F32)
    for zz in range(NZ):
        z_out[zz] = total[:, zz * 256 : (zz + 1) * 256].astype(BF16)
    for t in range(1, NZ):
        zz = (z + t) % NZ
        begin(rcopy(z_out.at[zz], z_in.at[z], z_s.at[zz], z_r.at[z], at_z(zz)))
    z_in[z] = z_out[z]

    scan_wait(1, suffix)

    def loop_f(h, _):
        cols = head(h)
        s = suffix[h]
        gk = dfk[:, cols] + dot(v_ref[:, cols], s, 1, 1)
        gk_ref[:, cols] = (gk * slope(k_ref[:, cols])).astype(BF16)
        gv_ref[:, cols] = (dgv[:, cols] + dot(fk[:, cols], s, 1, 0)).astype(BF16)
        return 0

    lax.fori_loop(0, 16, loop_f, 0, unroll=2)

    for t in range(1, NZ):
        zz = (z + t) % NZ
        rcopy(z_in.at[zz], z_in.at[zz], z_s.at[zz], z_r.at[zz], partner).wait_recv()
    whole = z_in[0].astype(F32)
    for zz in range(1, NZ):
        whole = whole + z_in[zz].astype(F32)
    f_out[...] = whole.astype(BF16)
    for t in range(8):
        to = final_to(t)

        @pl.when(jnp.logical_not(same(to)))
        def _(to=to, t=t):
            rcopy(f_out, f_in.at[z], f_s.at[t], f_r.at[z], to).start()

        @pl.when(same(to))
        def _():
            f_in[z] = f_out[...]

    for copy in pending:
        copy.wait_send()
    for t in range(8):
        to = final_to(t)

        @pl.when(jnp.logical_not(same(to)))
        def _(to=to, t=t):
            rcopy(f_out, f_in.at[z], f_s.at[t], f_r.at[z], to).wait_send()

    for zz in range(NZ):
        source = final_from(zz)

        @pl.when(jnp.logical_not(same(source)))
        def _(source=source, zz=zz):
            rcopy(f_in.at[zz], f_in.at[zz], f_s.at[zz], f_r.at[zz], source).wait_recv()

        gw_ref[:, zz * 256 : (zz + 1) * 256] = f_in[zz].astype(F32) * loss_scale


def on_device(loss_scale, query_rows, key_rows, value_rows, norm_gain, out_weight, cotangent):
    length, width = query_rows.shape[1:]
    rows = out_weight.shape[0]
    vmem = pl.BlockSpec(memory_space=pltpu.VMEM)
    block = jax.ShapeDtypeStruct((length, width), BF16)
    dma = pltpu.SemaphoreType.DMA
    states = (16, HEAD, HEAD)
    scratch = [
        pltpu.VMEM((length, width), BF16),
        pltpu.VMEM((length, width), BF16),
        pltpu.VMEM(states, BF16),
        pltpu.VMEM((length, width), F32),
        pltpu.VMEM((length, width), F32),
        pltpu.VMEM((length, width), BF16),
        pltpu.VMEM((length, width), BF16),
        pltpu.VMEM((length, width), F32),
        pltpu.VMEM((length, width), F32),
        pltpu.VMEM(states, F32),
        pltpu.VMEM((8, HEAD), F32),
        pltpu.VMEM((2, 8, HEAD, HEAD), BF16),
        pltpu.VMEM((2, 8, HEAD, HEAD), BF16),
        pltpu.VMEM((2, CHIPS, 64, HEAD), BF16),
        pltpu.VMEM((2, CHIPS, 64, HEAD), BF16),
        pltpu.VMEM((2, CHIPS, 64, HEAD), BF16),
        pltpu.VMEM((2, CHIPS, 64, HEAD), BF16),
        pltpu.VMEM((2, 8, HEAD, HEAD), BF16),
        pltpu.VMEM(states, BF16),
        pltpu.VMEM(states, BF16),
        pltpu.VMEM((32, 64, width), BF16),
        pltpu.VMEM((8, length, width), BF16),
        pltpu.VMEM((8, length, 256), BF16),
        pltpu.VMEM((4, 64, width), F32),
        pltpu.VMEM((4, 64, width), BF16),
        pltpu.VMEM((2, 64, HALF), BF16),
        pltpu.VMEM((2, 64, width), BF16),
        pltpu.VMEM((2, 64, width), BF16),
        pltpu.VMEM((8, 64, 256), BF16),
        pltpu.VMEM((8, 64, 256), BF16),
        pltpu.VMEM((64, 256), BF16),
        pltpu.VMEM((8, 64, 256), BF16),
        dma((2,)), dma((2,)), dma((2, 16)), dma((2, 16)), dma((2, 16)), dma((2, 16)), dma((2,)), dma((2,)),
        dma((4,)), dma((4,)), dma((4,)), dma((4,)), dma((8, 2)), dma((8, 2)), dma((16,)), dma((16,)),
        dma((2,)), dma((2,)), dma((2,)), dma((2,)), dma((4,)), dma((4,)),
        dma((8,)), dma((8,)), dma((2,)), dma((2,)), dma((2,)), dma((2,)), dma((8,)), dma((8,)), dma((8,)), dma((8,)),
    ]

    def body(*refs):
        kernel(loss_scale, *refs)

    mixed, gq, gk, gv, gw = pl.pallas_call(
        body,
        out_shape=(block, block, block, block, jax.ShapeDtypeStruct((rows, width), F32)),
        in_specs=[vmem] * 6,
        out_specs=(vmem,) * 5,
        scratch_shapes=scratch,
        compiler_params=pltpu.CompilerParams(
            collective_id=0, has_side_effects=True, vmem_limit_bytes=60 * 1024 * 1024
        ),
        name="layer",
    )(query_rows[0], key_rows[0], value_rows[0], norm_gain.reshape(1, width), out_weight, cotangent[0])
    return mixed[None], gq[None], gk[None], gv[None], gw


def solution(mesh):
    positions = mesh.shape["dp"] * mesh.shape["ctx"] * HEAD
    loss_scale = 1.0 / math.sqrt(positions)

    def run(*args):
        return on_device(loss_scale, *args)

    split = P("dp", "ctx", None)
    return jax.shard_map(
        run,
        mesh=mesh,
        in_specs=(split, split, split, P(), P("ctx", None), split),
        out_specs=(split, split, split, split, P("ctx", None)),
        check_vma=False,
    )
```

time: 678 us -> 131 us (0.19)
  the two profiles are of different devices: /device:TPU:1 before, /device:TPU:6 now
where the time goes in v1:
time: 131 us; the launch traced here: 130 us
  Pallas kernels  123 us (94%)
  local copies, waits for them, and re-layouts  6.42 us (5%)
    pallas_call x1, Pallas kernels, on_device(): pl.pallas_call(body, out_shape=(block, block, block, block, jax.ShapeDtyp...  123 us
    unnamed x13, local copies, waits for them, and re-layouts  6.42 us

profile of v1, /device:TPU:6, one launch (start us, length us, event | category | flops | bytes accessed | tf_op | source)
XLA Modules:
  0.0 130.4 jit_solution(12533269221321343508)
XLA Ops:
  0.6 123.4 %layer.1 = (bf16[128,2048]{1,0:T(8,128)(2,1)}, bf16[128,2048]{1,0:T(8,128)(2,1)}, bf16[128,2048]{1,0:T(8,128)(2,1)}, bf16[128,2048]{1,0:T(8,128)(2,1)}, f32[64,2048]{1,0:T(8,128)}) custom-call(bf16[128,2048]{1,0:T(8,128)(2,1)} %bitcast.13, bf16[128,2048]{1,0:T(8,128)(2,1)} %bitcast.14, bf16[128,2048]{1,0:T(8,128)(2,1)} %bitcast.15, f32[1,2048]{1,0:T(1,128)} %bitcast.17, ...), custom_call_target="tpu_custom_call" | custom-call | tf_op jit(solution)/shard_map/layer/pallas_call | solution.py:562
  124.0 0.0 copy-start.3
  124.0 1.9 %copy.16 = bf16[1,128,2048]{2,1,0:T(8,128)(2,1)} copy(bf16[1,128,2048]{2,1,0:T(8,128)(2,1)} %bitcast.12) | data formatting | bytes 1048576
  126.0 0.0 copy-done.3
  126.0 0.0 copy-start.2
  126.0 0.8 copy.17
  126.8 0.4 copy-done.2
  127.2 0.0 copy-start.1
  127.2 0.8 copy.18
  128.0 0.4 copy-done.1
  128.4 0.0 copy-start
  128.4 0.8 copy.19
  129.2 0.4 copy-done
  129.7 0.8 copy.20
Async XLA Ops:
  124.0 2.0 %copy-start.3 = (bf16[128,2048]{1,0:T(8,128)(2,1)S(1)}, bf16[128,2048]{1,0:T(8,128)(2,1)}, u32[]{:S(2)}) copy-start(bf16[128,2048]{1,0:T(8,128)(2,1)} %get-tuple-element.11) | copy-start | bytes 1572868
  126.0 1.2 copy-start.2
  127.2 1.2 copy-start.1
  128.4 1.2 copy-start

commit v2 on v1

--- a/solution.py
+++ b/solution.py
@@ -17,6 +17,9 @@
 NY = 4
 CHIPS = 16
 HALF = 1024
+CHUNKS = 2
+CHUNK = 2048 // CHUNKS
+PIECE = CHUNK // NZ
 
 
 def dot(a, b, ca, cb):
@@ -45,9 +48,10 @@
 
 def kernel(
     loss_scale,
-    q_ref, k_ref, v_ref, gain_ref, w_ref, cot_ref,
+    q_hbm, k_hbm, v_hbm, gain_ref, w_hbm, cot_hbm,
     mixed_ref, gq_ref, gk_ref, gv_ref, gw_ref,
-    fq, fk, probs, att, dnorm, normed, datt, dfk, dgv, local, state,
+    q_ref, k_ref, v_ref, w_ref, cot_ref, in_s,
+    fq, fk, probs, att, dnorm, normed, datt, dfk, dgv, local, inverse,
     xsend, xrecv, pieces, got, back_out, back_in, psend, prefix, suffix,
     wfull, cotg, normg, gwf, gwt, xh_in, x_out, x_in, z_out, z_in, f_out, f_in,
     sx_s, sx_r, s1_s, s1_r, s2_s, s2_r, sp_s, sp_r,
@@ -92,6 +96,11 @@
     def same(device):
         return jnp.logical_and(device[0] == d, device[1] == i)
 
+    inputs = ((k_hbm, k_ref), (v_hbm, v_ref), (q_hbm, q_ref), (w_hbm, w_ref), (cot_hbm, cot_ref))
+    loads = [pltpu.make_async_copy(a, b, in_s.at[n]) for n, (a, b) in enumerate(inputs)]
+    for load in loads:
+        load.start()
+
     barrier = pltpu.get_barrier_semaphore()
 
     def greet(device):
@@ -125,7 +134,11 @@
         local[h] = dot(kf, v_ref[:, cols], 0, 0)
         return 0
 
+    for load in loads[:3]:
+        load.wait()
     lax.fori_loop(0, 16, loop_a, 0, unroll=2)
+    for load in loads[3:]:
+        load.wait()
 
     selves = jnp.where(8 * y + 4 * c + x == i, 2, 0)
     pl.semaphore_wait(barrier, 15 + 1 + 3 + 6 + 16 - selves)
@@ -314,10 +327,113 @@
         ref = out.at[other_heads]
         rcopy(ref, ref, sp_s.at[n], sp_r.at[n], partner).wait_recv()
 
-    scan_pair(0)
-    w_first()
-    c_first()
-    scan_spread(0)
+    me8 = y * 2 + c
+
+    def block8(b):
+        return pl.ds(pl.multiple_of(b * 256, 256), 256)
+
+    def n_send():
+        for t in range(1, 8):
+            b = (me8 + t) % 8
+            begin(
+                rcopy(
+                    normed.at[:, block8(b)], normg.at[me8], n_s.at[b], n_r.at[me8], at_y(b // 2, b % 2)
+                )
+            )
+        normg[me8] = normed[:, block8(me8)]
+
+    def n_wait():
+        for t in range(1, 8):
+            b = (me8 + t) % 8
+            ref = normg.at[b]
+            rcopy(ref, ref, n_s.at[b], n_r.at[b], partner).wait_recv()
+
+    x_up = at_x((x + 1) % NX)
+    x_dn = at_x((x + 3) % NX)
+    two = (x + 2) % NX
+    one_up = (x + 1) % NX
+    one_dn = (x + 3) % NX
+
+    def part(h, lo, size):
+        return pl.ds(h * CHUNK + lo, size)
+
+    def g_tile(h):
+        def loop_g(n, _):
+            cols = pl.ds(pl.multiple_of(h * CHUNK + n * 512, 512), 512)
+            tile = dot(normg[...].reshape(1024, 256), cotg[:, :, cols].reshape(1024, 512), 0, 0)
+            gwf[:, :, cols] = tile.reshape(4, 64, 512)
+            gwt[:, :, cols] = tile.astype(BF16).reshape(4, 64, 512)
+            return 0
+
+        lax.fori_loop(0, CHUNK // 512, loop_g, 0)
+
+    def g_first(h):
+        low, high = part(h, 0, CHUNK // 2), part(h, CHUNK // 2, CHUNK // 2)
+        begin(rcopy(gwt.at[two, :, low], xh_in.at[h, 0], xa_s.at[h, 0], xa_r.at[h, 0], x_up))
+        begin(rcopy(gwt.at[two, :, high], xh_in.at[h, 1], xa_s.at[h, 1], xa_r.at[h, 1], x_dn))
+
+    def g_second(h):
+        low, high = part(h, 0, CHUNK // 2), part(h, CHUNK // 2, CHUNK // 2)
+        lows, highs = pl.ds(0, CHUNK // 2), pl.ds(CHUNK // 2, CHUNK // 2)
+        for a, to in ((0, x_up), (1, x_dn)):
+            rcopy(xh_in.at[h, a], xh_in.at[h, a], xa_s.at[h, a], xa_r.at[h, a], to).wait_recv()
+        x_out[h, 0, :, lows] = (gwf[one_up, :, low] + xh_in[h, 0].astype(F32)).astype(BF16)
+        x_out[h, 0, :, highs] = gwt[one_up, :, high]
+        x_out[h, 1, :, lows] = gwt[one_dn, :, low]
+        x_out[h, 1, :, highs] = (gwf[one_dn, :, high] + xh_in[h, 1].astype(F32)).astype(BF16)
+        begin(rcopy(x_out.at[h, 0], x_in.at[h, 0], xb_s.at[h, 0], xb_r.at[h, 0], x_up))
+        begin(rcopy(x_out.at[h, 1], x_in.at[h, 1], xb_s.at[h, 1], xb_r.at[h, 1], x_dn))
+
+    def g_third(h):
+        for a, to in ((0, x_up), (1, x_dn)):
+            rcopy(x_in.at[h, a], x_in.at[h, a], xb_s.at[h, a], xb_r.at[h, a], to).wait_recv()
+        total = gwf[x, :, part(h, 0, CHUNK)] + x_in[h, 0].astype(F32) + x_in[h, 1].astype(F32)
+        for zz in range(NZ):
+            z_out[h, zz] = total[:, zz * PIECE : (zz + 1) * PIECE].astype(BF16)
+        for t in range(1, NZ):
+            zz = (z + t) % NZ
+            begin(rcopy(z_out.at[h, zz], z_in.at[h, z], z_s.at[h, zz], z_r.at[h, z], at_z(zz)))
+        z_in[h, z] = z_out[h, z]
+
+    def f_copy(h, t):
+        return rcopy(f_out.at[h], f_in.at[h, z], f_s.at[h, t], f_r.at[h, z], final_to(t))
+
+    def g_fourth(h):
+        for t in range(1, NZ):
+            zz = (z + t) % NZ
+            ref = z_in.at[h, zz]
+            rcopy(ref, ref, z_s.at[h, zz], z_r.at[h, zz], partner).wait_recv()
+        whole = z_in[h, 0].astype(F32)
+        for zz in range(1, NZ):
+            whole = whole + z_in[h, zz].astype(F32)
+        f_out[h] = whole.astype(BF16)
+        for t in range(8):
+            to = final_to(t)
+
+            @pl.when(jnp.logical_not(same(to)))
+            def _(t=t):
+                f_copy(h, t).start()
+
+            @pl.when(same(to))
+            def _():
+                f_in[h, z] = f_out[h]
+
+    def g_end(h):
+        for zz in range(NZ):
+            source = final_from(zz)
+
+            @pl.when(jnp.logical_not(same(source)))
+            def _(source=source, zz=zz):
+                ref = f_in.at[h, zz]
+                rcopy(ref, ref, f_s.at[h, zz], f_r.at[h, zz], source).wait_recv()
+
+            gw_ref[:, h * CHUNK + zz * PIECE : h * CHUNK + (zz + 1) * PIECE] = f_in[h, zz].astype(F32) * loss_scale
+        for t in range(8):
+            to = final_to(t)
+
+            @pl.when(jnp.logical_not(same(to)))
+            def _(t=t):
+                f_copy(h, t).wait_send()
 
     rows_at = lax.broadcasted_iota(jnp.int32, (HEAD, HEAD), 0)
     cols_at = lax.broadcasted_iota(jnp.int32, (HEAD, HEAD), 1)
@@ -331,137 +447,48 @@
         att[:, cols] = dot(p, v_ref[:, cols], 1, 0)
         return 0
 
-    lax.fori_loop(0, 16, loop_b, 0, unroll=2)
-    wfull[i] = w_ref[...]
-    cotg[cslot(0)] = cot_ref[...]
-
-    w_step(1)
-    scan_return(0)
-    w_other(0)
-    w_step(2)
-    c_second()
-    scan_share(0, prefix)
-    w_other(7)
-    w_other(1)
-    w_step(3)
-    scan_wait(0, prefix)
-    w_other(6)
-    w_other(2)
-    w_last()
-    c_third()
-    for r in (5, 3, 4):
-        w_other(r)
-    w_pair_wait()
-
     def loop_c(h2, _):
         cols = pl.ds(pl.multiple_of(h2 * 256, 256), 256)
         rows = wfull[pl.ds(h2 * 4, 4)].reshape(256, 2048)
         dnorm[:, cols] = dot(cot_ref[...], rows, 1, 1) * gain_ref[:, cols]
         return 0
 
-    lax.fori_loop(0, 8, loop_c, 0)
+    def loop_n(h, _):
+        cols = head(h)
+        a = att[:, cols] + dot(fq[:, cols], prefix[h], 1, 0)
+        inv = lax.rsqrt(jnp.mean(a * a, axis=-1, keepdims=True) + EPSILON)
+        att[:, cols] = a
+        inverse[h] = inv
+        normed[:, cols] = (a * inv * gain_ref[:, cols]).astype(BF16)
+        return 0
 
     def loop_d(h, _):
         cols = head(h)
-        fqh = fq[:, cols]
-        a = att[:, cols] + dot(fqh, prefix[h], 1, 0)
-        inverse = lax.rsqrt(jnp.mean(a * a, axis=-1, keepdims=True) + EPSILON)
-        ai = a * inverse
-        normed[:, cols] = (ai * gain_ref[:, cols]).astype(BF16)
+        a = att[:, cols]
+        inv = inverse[h]
         s = dnorm[:, cols]
         m = jnp.mean(s * a, axis=-1, keepdims=True)
-        g = (inverse * (s - ai * inverse * m)).astype(BF16)
+        g = (inv * (s - a * inv * inv * m)).astype(BF16)
         datt[:, cols] = g
-        local[h] = dot(fqh, g, 0, 0)
-        return 0
-
-    lax.fori_loop(0, 16, loop_d, 0, unroll=2)
-
-    me8 = y * 2 + c
-
-    def block8(b):
-        return pl.ds(pl.multiple_of(b * 256, 256), 256)
-
-    scan_pair(1)
-    for t in range(1, 8):
-        b = (me8 + t) % 8
-        begin(
-            rcopy(
-                normed.at[:, block8(b)], normg.at[me8], n_s.at[b], n_r.at[me8], at_y(b // 2, b % 2)
-            )
-        )
-    normg[me8] = normed[:, block8(me8)]
-    scan_spread(1)
+        local[h] = dot(fq[:, cols], g, 0, 0)
+        return 0
 
     def loop_e(h, _):
         cols = head(h)
         g = datt[:, cols]
-        vh = v_ref[:, cols]
         fkh = fk[:, cols]
-        fqh = fq[:, cols]
-        dp = jnp.where(causal, dot(g, vh, 1, 1), 0.0).astype(BF16)
+        dp = jnp.where(causal, dot(g, v_ref[:, cols], 1, 1), 0.0).astype(BF16)
         dfq = dot(dp, fkh, 1, 0) + dot(g, prefix[h], 1, 1)
         gq_ref[:, cols] = (dfq * slope(q_ref[:, cols])).astype(BF16)
-        dfk[:, cols] = dot(dp, fqh, 0, 0)
+        dfk[:, cols] = dot(dp, fq[:, cols], 0, 0)
         dgv[:, cols] = dot(probs[h], g, 0, 0)
         return 0
-
-    lax.fori_loop(0, 16, loop_e, 0, unroll=2)
-
-    c_wait()
-    for t in range(1, 8):
-        b = (me8 + t) % 8
-        ref = normg.at[b]
-        rcopy(ref, ref, n_s.at[b], n_r.at[b], partner).wait_recv()
-
-    def loop_g(n, _):
-        cols = pl.ds(pl.multiple_of(n * 512, 512), 512)
-        a = normg[...].reshape(1024, 256)
-        b = cotg[:, :, cols].reshape(1024, 512)
-        tile = dot(a, b, 0, 0)
-        gwf[:, :, cols] = tile.reshape(4, 64, 512)
-        gwt[:, :, cols] = tile.astype(BF16).reshape(4, 64, 512)
-        return 0
-
-    lax.fori_loop(0, 4, loop_g, 0)
-
-    x_up = at_x((x + 1) % NX)
-    x_dn = at_x((x + 3) % NX)
-    two = (x + 2) % NX
-    begin(rcopy(gwt.at[two, :, left], xh_in.at[0], xa_s.at[0], xa_r.at[0], x_up))
-    begin(rcopy(gwt.at[two, :, right], xh_in.at[1], xa_s.at[1], xa_r.at[1], x_dn))
-    scan_return(1)
-    for a, to in ((0, x_up), (1, x_dn)):
-        rcopy(xh_in.at[a], xh_in.at[a], xa_s.at[a], xa_r.at[a], to).wait_recv()
-    one_up = (x + 1) % NX
-    one_dn = (x + 3) % NX
-    x_out[0, :, left] = (gwf[one_up, :, left] + xh_in[0].astype(F32)).astype(BF16)
-    x_out[0, :, right] = gwt[one_up, :, right]
-    x_out[1, :, left] = gwt[one_dn, :, left]
-    x_out[1, :, right] = (gwf[one_dn, :, right] + xh_in[1].astype(F32)).astype(BF16)
-    begin(rcopy(x_out.at[0], x_in.at[0], xb_s.at[0], xb_r.at[0], x_up))
-    begin(rcopy(x_out.at[1], x_in.at[1], xb_s.at[1], xb_r.at[1], x_dn))
 
     def loop_m(n, _):
         cols = pl.ds(pl.multiple_of(n * 512, 512), 512)
         rows = wfull[:, :, cols].reshape(2048, 512)
         mixed_ref[:, cols] = dot(normed[...], rows, 1, 0).astype(BF16)
         return 0
-
-    lax.fori_loop(0, 4, loop_m, 0)
-
-    scan_share(1, suffix)
-    for a, to in ((0, x_up), (1, x_dn)):
-        rcopy(x_in.at[a], x_in.at[a], xb_s.at[a], xb_r.at[a], to).wait_recv()
-    total = gwf[x] + x_in[0].astype(F32) + x_in[1].astype(F32)
-    for zz in range(NZ):
-        z_out[zz] = total[:, zz * 256 : (zz + 1) * 256].astype(BF16)
-    for t in range(1, NZ):
-        zz = (z + t) % NZ
-        begin(rcopy(z_out.at[zz], z_in.at[z], z_s.at[zz], z_r.at[z], at_z(zz)))
-    z_in[z] = z_out[z]
-
-    scan_wait(1, suffix)
 
     def loop_f(h, _):
         cols = head(h)
@@ -471,55 +498,85 @@
         gv_ref[:, cols] = (dgv[:, cols] + dot(fk[:, cols], s, 1, 0)).astype(BF16)
         return 0
 
+    scan_pair(0)
+    w_first()
+    c_first()
+    scan_spread(0)
+    lax.fori_loop(0, 16, loop_b, 0, unroll=2)
+    wfull[i] = w_ref[...]
+    cotg[cslot(0)] = cot_ref[...]
+    scan_return(0)
+    w_step(1)
+    w_other(0)
+    c_second()
+    scan_share(0, prefix)
+    scan_wait(0, prefix)
+    w_step(2)
+    lax.fori_loop(0, 16, loop_n, 0, unroll=2)
+    n_send()
+    w_other(7)
+    w_other(1)
+    c_third()
+    w_step(3)
+    c_wait()
+    n_wait()
+    for h in range(CHUNKS):
+        g_tile(h)
+        g_first(h)
+    w_other(6)
+    w_other(2)
+    w_last()
+    for h in range(CHUNKS):
+        g_second(h)
+    for r in (5, 3, 4):
+        w_other(r)
+    w_pair_wait()
+    lax.fori_loop(0, 8, loop_c, 0)
+    lax.fori_loop(0, 16, loop_d, 0, unroll=2)
+    scan_pair(1)
+    g_third(0)
+    scan_spread(1)
+    for h in range(1, CHUNKS):
+        g_third(h)
+    lax.fori_loop(0, 16, loop_e, 0, unroll=2)
+    scan_return(1)
+    for h in range(CHUNKS):
+        g_fourth(h)
+    lax.fori_loop(0, 4, loop_m, 0)
+    scan_share(1, suffix)
+    scan_wait(1, suffix)
     lax.fori_loop(0, 16, loop_f, 0, unroll=2)
-
-    for t in range(1, NZ):
-        zz = (z + t) % NZ
-        rcopy(z_in.at[zz], z_in.at[zz], z_s.at[zz], z_r.at[zz], partner).wait_recv()
-    whole = z_in[0].astype(F32)
-    for zz in range(1, NZ):
-        whole = whole + z_in[zz].astype(F32)
-    f_out[...] = whole.astype(BF16)
-    for t in range(8):
-        to = final_to(t)
-
-        @pl.when(jnp.logical_not(same(to)))
-        def _(to=to, t=t):
-            rcopy(f_out, f_in.at[z], f_s.at[t], f_r.at[z], to).start()
-
-        @pl.when(same(to))
-        def _():
-            f_in[z] = f_out[...]
-
     for copy in pending:
         copy.wait_send()
-    for t in range(8):
-        to = final_to(t)
-
-        @pl.when(jnp.logical_not(same(to)))
-        def _(to=to, t=t):
-            rcopy(f_out, f_in.at[z], f_s.at[t], f_r.at[z], to).wait_send()
-
-    for zz in range(NZ):
-        source = final_from(zz)
-
-        @pl.when(jnp.logical_not(same(source)))
-        def _(source=source, zz=zz):
-            rcopy(f_in.at[zz], f_in.at[zz], f_s.at[zz], f_r.at[zz], source).wait_recv()
-
-        gw_ref[:, zz * 256 : (zz + 1) * 256] = f_in[zz].astype(F32) * loss_scale
+    for h in range(CHUNKS):
+        g_end(h)
+
+
+def finish(*refs):
+    copies = [pltpu.make_async_copy(refs[n], refs[5 + n], refs[10].at[n]) for n in range(5)]
+    for copy in copies:
+        copy.start()
+    for copy in copies:
+        copy.wait()
 
 
 def on_device(loss_scale, query_rows, key_rows, value_rows, norm_gain, out_weight, cotangent):
     length, width = query_rows.shape[1:]
     rows = out_weight.shape[0]
     vmem = pl.BlockSpec(memory_space=pltpu.VMEM)
+    hbm = pl.BlockSpec(memory_space=pltpu.HBM)
     block = jax.ShapeDtypeStruct((length, width), BF16)
     dma = pltpu.SemaphoreType.DMA
     states = (16, HEAD, HEAD)
     scratch = [
         pltpu.VMEM((length, width), BF16),
         pltpu.VMEM((length, width), BF16),
+        pltpu.VMEM((length, width), BF16),
+        pltpu.VMEM((rows, width), BF16),
+        pltpu.VMEM((length, width), BF16),
+        dma((5,)),
+        pltpu.VMEM((length, width), BF16),
+        pltpu.VMEM((length, width), BF16),
         pltpu.VMEM(states, BF16),
         pltpu.VMEM((length, width), F32),
         pltpu.VMEM((length, width), F32),
@@ -528,7 +585,7 @@
         pltpu.VMEM((length, width), F32),
         pltpu.VMEM((length, width), F32),
         pltpu.VMEM(states, F32),
-        pltpu.VMEM((8, HEAD), F32),
+        pltpu.VMEM((16, length, 1), F32),
         pltpu.VMEM((2, 8, HEAD, HEAD), BF16),
         pltpu.VMEM((2, 8, HEAD, HEAD), BF16),
         pltpu.VMEM((2, CHIPS, 64, HEAD), BF16),
@@ -543,33 +600,46 @@
         pltpu.VMEM((8, length, 256), BF16),
         pltpu.VMEM((4, 64, width), F32),
         pltpu.VMEM((4, 64, width), BF16),
-        pltpu.VMEM((2, 64, HALF), BF16),
-        pltpu.VMEM((2, 64, width), BF16),
-        pltpu.VMEM((2, 64, width), BF16),
-        pltpu.VMEM((8, 64, 256), BF16),
-        pltpu.VMEM((8, 64, 256), BF16),
-        pltpu.VMEM((64, 256), BF16),
-        pltpu.VMEM((8, 64, 256), BF16),
+        pltpu.VMEM((CHUNKS, 2, 64, CHUNK // 2), BF16),
+        pltpu.VMEM((CHUNKS, 2, 64, CHUNK), BF16),
+        pltpu.VMEM((CHUNKS, 2, 64, CHUNK), BF16),
+        pltpu.VMEM((CHUNKS, 8, 64, PIECE), BF16),
+        pltpu.VMEM((CHUNKS, 8, 64, PIECE), BF16),
+        pltpu.VMEM((CHUNKS, 64, PIECE), BF16),
+        pltpu.VMEM((CHUNKS, 8, 64, PIECE), BF16),
         dma((2,)), dma((2,)), dma((2, 16)), dma((2, 16)), dma((2, 16)), dma((2, 16)), dma((2,)), dma((2,)),
         dma((4,)), dma((4,)), dma((4,)), dma((4,)), dma((8, 2)), dma((8, 2)), dma((16,)), dma((16,)),
         dma((2,)), dma((2,)), dma((2,)), dma((2,)), dma((4,)), dma((4,)),
-        dma((8,)), dma((8,)), dma((2,)), dma((2,)), dma((2,)), dma((2,)), dma((8,)), dma((8,)), dma((8,)), dma((8,)),
+        dma((8,)), dma((8,)),
+        dma((CHUNKS, 2)), dma((CHUNKS, 2)), dma((CHUNKS, 2)), dma((CHUNKS, 2)),
+        dma((CHUNKS, 8)), dma((CHUNKS, 8)), dma((CHUNKS, 8)), dma((CHUNKS, 8)),
     ]
 
     def body(*refs):
         kernel(loss_scale, *refs)
 
-    mixed, gq, gk, gv, gw = pl.pallas_call(
+    shapes = (block, block, block, block, jax.ShapeDtypeStruct((rows, width), F32))
+    results = pl.pallas_call(
         body,
-        out_shape=(block, block, block, block, jax.ShapeDtypeStruct((rows, width), F32)),
-        in_specs=[vmem] * 6,
+        out_shape=shapes,
+        in_specs=[hbm, hbm, hbm, vmem, hbm, hbm],
         out_specs=(vmem,) * 5,
         scratch_shapes=scratch,
         compiler_params=pltpu.CompilerParams(
-            collective_id=0, has_side_effects=True, vmem_limit_bytes=60 * 1024 * 1024
+            collective_id=0, has_side_effects=True, vmem_limit_bytes=44 * 1024 * 1024
         ),
         name="layer",
     )(query_rows[0], key_rows[0], value_rows[0], norm_gain.reshape(1, width), out_weight, cotangent[0])
+    anywhere = pl.BlockSpec(memory_space=pl.ANY)
+    mixed, gq, gk, gv, gw = pl.pallas_call(
+        finish,
+        out_shape=shapes,
+        in_specs=[anywhere] * 5,
+        out_specs=(hbm,) * 5,
+        scratch_shapes=[dma((5,))],
+        compiler_params=pltpu.CompilerParams(vmem_limit_bytes=8 * 1024 * 1024),
+        name="finish",
+    )(*results)
     return mixed[None], gq[None], gk[None], gv[None], gw
 
 

time: 131 us -> 118 us (0.901)
  the two profiles are of different devices: /device:TPU:6 before, /device:TPU:56 now
where the time goes in v2:
time: 118 us
  Pallas kernels  111 us (94%)
  local copies, waits for them, and re-layouts  5.8 us (5%)
    pallas_call x1, Pallas kernels, on_device(): pl.pallas_call(body, out_shape=shapes, in_specs=[hbm, hbm, hbm, vmem, hbm...  110 us
    unnamed x12, local copies, waits for them, and re-layouts  5.8 us

profile of v2, /device:TPU:56, one launch (start us, length us, event | category | flops | bytes accessed | tf_op | source)
XLA Modules:
  0.0 117.8 jit_solution(492208782513902831)
XLA Ops:
  0.6 0.0 copy-start.5
  0.6 0.7 copy-done.5
  1.3 0.0 copy-start
  1.3 1.0 copy-done
  2.4 0.0 copy-start.1
  2.4 1.0 copy-done.1
  3.4 0.0 copy-start.2
  3.4 1.0 copy-done.2
  4.5 0.0 copy-start.3
  4.5 1.0 copy-done.3
  5.5 0.0 copy-start.4
  5.5 0.9 copy-done.4
  6.5 109.8 %layer.1 = (bf16[128,2048]{1,0:T(8,128)(2,1)S(1)}, bf16[128,2048]{1,0:T(8,128)(2,1)S(1)}, bf16[128,2048]{1,0:T(8,128)(2,1)S(1)}, bf16[128,2048]{1,0:T(8,128)(2,1)S(1)}, f32[64,2048]{1,0:T(8,128)S(1)}) custom-call(bf16[128,2048]{1,0:T(8,128)(2,1)S(1)} %bitcast.9, bf16[128,2048]{1,0:T(8,128)(2,1)S(1)} %bitcast.10, bf16[128,2048]{1,0:T(8,128)(2,1)S(1)} %bitcast.11, ...), custom_call_target="tpu_custom_call" | custom-call | tf_op jit(solution)/shard_map/layer/pallas_call | solution.py:622
  116.3 1.5 %finish.1 = (bf16[128,2048]{1,0:T(8,128)(2,1)}, bf16[128,2048]{1,0:T(8,128)(2,1)}, bf16[128,2048]{1,0:T(8,128)(2,1)}, bf16[128,2048]{1,0:T(8,128)(2,1)}, f32[64,2048]{1,0:T(8,128)}) custom-call(bf16[128,2048]{1,0:T(8,128)(2,1)S(1)} %get-tuple-element.15.refs_0_, bf16[128,2048]{1,0:T(8,128)(2,1)S(1)} %get-tuple-element.16.refs_1_, ...), custom_call_target="tpu_custom_call" | custom-call | tf_op jit(solution)/shard_map/finish/pallas_call | solution.py:634
Async XLA Ops:
  0.6 0.7 copy-start.5
  1.3 1.0 copy-start
  2.4 1.0 copy-start.1
  3.4 1.0 copy-start.2
  4.5 1.0 copy-start.3
  5.5 0.9 copy-start.4

commit v3 on v2

--- a/solution.py
+++ b/solution.py
@@ -19,7 +19,7 @@
 HALF = 1024
 CHUNKS = 2
 CHUNK = 2048 // CHUNKS
-PIECE = CHUNK // NZ
+WIDE = CHUNK // 2
 
 
 def dot(a, b, ca, cb):
@@ -48,14 +48,14 @@
 
 def kernel(
     loss_scale,
-    q_hbm, k_hbm, v_hbm, gain_ref, w_hbm, cot_hbm,
+    q_hbm, k_hbm, v_hbm, gain_hbm, w_hbm, cot_hbm,
     mixed_ref, gq_ref, gk_ref, gv_ref, gw_ref,
-    q_ref, k_ref, v_ref, w_ref, cot_ref, in_s,
+    q_ref, k_ref, v_ref, gain_ref, w_ref, cot_ref, in_s,
     fq, fk, probs, att, dnorm, normed, datt, dfk, dgv, local, inverse,
     xsend, xrecv, pieces, got, back_out, back_in, psend, prefix, suffix,
-    wfull, cotg, normg, gwf, gwt, xh_in, x_out, x_in, z_out, z_in, f_out, f_in,
+    wfull, cotg, flipped, normg, gwf, gwt, xh_in, x_out, x_in, z_out, z_in, f_out, f_in,
     sx_s, sx_r, s1_s, s1_r, s2_s, s2_r, sp_s, sp_r,
-    up_s, up_r, dn_s, dn_r, wx_s, wx_r, wp_s, wp_r,
+    up_s, up_r, dn_s, dn_r, wx_s, wx_r, wy_s, wy_r, wp_s, wp_r,
     cu_s, cu_r, cd_s, cd_r, cp_s, cp_r,
     n_s, n_r, xa_s, xa_r, xb_s, xb_r, z_s, z_r, f_s, f_r,
 ):
@@ -84,19 +84,15 @@
         return (yy * 2 + xh, j * 2 + cc)
 
     def final_to(t):
-        return (t, 8 * y + 4 * c + x)
-
-    from_x = i % 4
-    from_c = (i // 4) % 2
-    from_d = (i // 8) * 2 + from_x // 2
-
-    def final_from(zz):
-        return (from_d, ((from_x % 2) * NZ + zz) * 2 + from_c)
+        return (t, (xl * NZ + z) * 2 + y // 2)
+
+    def final_from(t):
+        return ((2 * c + t // 4) * 2 + t % 2, (xl * NZ + z) * 2 + (t // 2) % 2)
 
     def same(device):
         return jnp.logical_and(device[0] == d, device[1] == i)
 
-    inputs = ((k_hbm, k_ref), (v_hbm, v_ref), (q_hbm, q_ref), (w_hbm, w_ref), (cot_hbm, cot_ref))
+    inputs = ((k_hbm, k_ref), (v_hbm, v_ref), (q_hbm, q_ref), (w_hbm, w_ref), (cot_hbm, cot_ref), (gain_hbm, gain_ref))
     loads = [pltpu.make_async_copy(a, b, in_s.at[n]) for n, (a, b) in enumerate(inputs)]
     for load in loads:
         load.start()
@@ -140,7 +136,7 @@
     for load in loads[3:]:
         load.wait()
 
-    selves = jnp.where(8 * y + 4 * c + x == i, 2, 0)
+    selves = jnp.where(y // 2 == c, 2, 0)
     pl.semaphore_wait(barrier, 15 + 1 + 3 + 6 + 16 - selves)
 
     left = pl.ds(0, HALF)
@@ -164,72 +160,89 @@
     z_up = at_z((z + 1) % NZ)
     z_dn = at_z((z + NZ - 1) % NZ)
 
-    def wsrc(r, cols=None):
-        if r == 0:
-            return w_ref if cols is None else w_ref.at[:, cols]
-        slot = wslot((z + r) % NZ)
-        return wfull.at[slot] if cols is None else wfull.at[slot, :, cols]
-
-    def wdst(r, cols=None):
-        slot = wslot((z + r) % NZ)
-        return wfull.at[slot] if cols is None else wfull.at[slot, :, cols]
+    p = y % 2
+    mine_w = pl.ds(pl.multiple_of(p * HALF, HALF), HALF)
+    rest_w = pl.ds(pl.multiple_of((1 - p) * HALF, HALF), HALF)
+
+    def quarter(side, a):
+        return pl.ds(pl.multiple_of(side * HALF + a * 512, 512), 512)
+
+    y_up = at_y((y + 1) % NY, c)
+    y_dn = at_y((y + NY - 1) % NY, c)
+
+    def wcols(r, cols, own=False):
+        if r == 0 and not own:
+            return w_ref.at[:, cols]
+        return wfull.at[wslot((z + r) % NZ), :, cols]
+
+    def z_cols(k, a):
+        return quarter(p, a) if k == 3 else mine_w
 
     def w_up(k):
-        cols = left if k == 3 else None
         r = (-k) % NZ
-        return rcopy(wsrc(r, cols), wdst(r, cols), up_s.at[k], up_r.at[k], z_up)
+        cols = z_cols(k, 0)
+        begin(rcopy(wcols(r, cols), wcols(r, cols, True), up_s.at[k], up_r.at[k], z_up))
 
     def w_dn(k):
-        cols = right if k == 3 else None
-        return rcopy(wsrc(k, cols), wdst(k, cols), dn_s.at[k], dn_r.at[k], z_dn)
+        cols = z_cols(k, 1)
+        begin(rcopy(wcols(k, cols), wcols(k, cols, True), dn_s.at[k], dn_r.at[k], z_dn))
 
     def w_up_wait(k):
-        r = (-k - 1) % NZ
-        cols = left if k == 3 else None
-        ref = wdst(r, cols)
+        ref = wcols((-k - 1) % NZ, z_cols(k, 0), True)
         rcopy(ref, ref, up_s.at[k], up_r.at[k], z_up).wait_recv()
 
     def w_dn_wait(k):
-        cols = right if k == 3 else None
-        ref = wdst(k + 1, cols)
+        ref = wcols(k + 1, z_cols(k, 1), True)
         rcopy(ref, ref, dn_s.at[k], dn_r.at[k], z_dn).wait_recv()
 
     def w_near(r):
-        begin(rcopy(wsrc(r, left), wdst(r, left), wx_s.at[r, 0], wx_r.at[r, 0], near_x))
+        begin(rcopy(wcols(r, mine_w), wcols(r, mine_w, True), wx_s.at[r, 0], wx_r.at[r, 0], near_x))
 
     def w_far(r):
-        begin(rcopy(wsrc(r, right), wdst(r, right), wx_s.at[r, 1], wx_r.at[r, 1], far_x))
+        begin(rcopy(wcols(r, rest_w), wcols(r, rest_w, True), wx_s.at[r, 1], wx_r.at[r, 1], far_x))
 
     def w_pair(r):
-        begin(rcopy(wsrc(r), wdst(r), wp_s.at[r], wp_r.at[r], partner))
+        dst = wfull.at[wslot((z + r) % NZ)]
+        begin(rcopy(w_ref if r == 0 else dst, dst, wp_s.at[r], wp_r.at[r], partner))
+
+    def w_side(r, a):
+        ref = wcols(r, quarter(p, a))
+        begin(rcopy(ref, ref, wy_s.at[r, a], wy_r.at[r, a], y_dn if a else y_up))
 
     def w_first():
-        begin(w_up(0))
-        begin(w_dn(0))
+        w_up(0)
+        w_dn(0)
         w_near(0)
         w_far(0)
         w_pair(0)
 
     def w_step(k):
         w_up_wait(k - 1)
-        begin(w_up(k))
+        w_up(k)
         w_dn_wait(k - 1)
-        begin(w_dn(k))
+        w_dn(k)
         for r in ((-k) % NZ, k):
             w_near(r)
-            w_far(r)
-            w_pair(r)
+            w_side(r, 0)
+            w_side(r, 1)
 
     def w_last():
         w_up_wait(3)
+        w_side(4, 0)
+        w_dn_wait(3)
+        w_side(4, 1)
         w_near(4)
-        w_dn_wait(3)
-        w_far(4)
-        w_pair(4)
+
+    def w_rest(r):
+        for a in (0, 1):
+            ref = wcols(r, quarter(1 - p, a))
+            rcopy(ref, ref, wy_s.at[r, a], wy_r.at[r, a], y_up).wait_recv()
+        w_far(r)
+        w_pair(r)
 
     def w_other(r):
         slot = oslot((z + r) % NZ)
-        for a, cols in ((0, left), (1, right)):
+        for a, cols in ((0, mine_w), (1, rest_w)):
             ref = wfull.at[slot, :, cols]
             rcopy(ref, ref, wx_s.at[r, a], wx_r.at[r, a], near_x).wait_recv()
         begin(rcopy(wfull.at[slot], wfull.at[slot], wp_s.at[8 + r], wp_r.at[8 + r], partner))
@@ -240,9 +253,6 @@
             side = xl if r < 8 else 1 - xl
             ref = wfull.at[(side * NZ + zz) * 2 + o]
             rcopy(ref, ref, wp_s.at[r], wp_r.at[r], partner).wait_recv()
-
-    y_up = at_y((y + 1) % NY, c)
-    y_dn = at_y((y + NY - 1) % NY, c)
 
     def cslot(r):
         return ((y + r) % NY) * 2 + c
@@ -329,23 +339,27 @@
 
     me8 = y * 2 + c
 
-    def block8(b):
-        return pl.ds(pl.multiple_of(b * 256, 256), 256)
+    def positions(b):
+        return pl.ds(pl.multiple_of(b * HEAD, HEAD), HEAD)
 
     def n_send():
         for t in range(1, 8):
             b = (me8 + t) % 8
             begin(
                 rcopy(
-                    normed.at[:, block8(b)], normg.at[me8], n_s.at[b], n_r.at[me8], at_y(b // 2, b % 2)
+                    flipped.at[:, b],
+                    normg.at[:, :, positions(me8)],
+                    n_s.at[b],
+                    n_r.at[me8],
+                    at_y(b // 2, b % 2),
                 )
             )
-        normg[me8] = normed[:, block8(me8)]
+        normg[:, :, positions(me8)] = flipped[:, me8]
 
     def n_wait():
         for t in range(1, 8):
             b = (me8 + t) % 8
-            ref = normg.at[b]
+            ref = normg.at[:, :, positions(b)]
             rcopy(ref, ref, n_s.at[b], n_r.at[b], partner).wait_recv()
 
     x_up = at_x((x + 1) % NX)
@@ -354,49 +368,56 @@
     one_up = (x + 1) % NX
     one_dn = (x + 3) % NX
 
-    def part(h, lo, size):
-        return pl.ds(h * CHUNK + lo, size)
+    def piece(k, h, lo, size):
+        cols = pl.ds(pl.multiple_of(h * CHUNK + (k // 2) * WIDE + lo, HEAD), size)
+        return pl.ds(8 * (k % 2), 8), slice(None), cols
+
+    lows, highs = pl.ds(0, WIDE // 2), pl.ds(WIDE // 2, WIDE // 2)
+
+    def low(k, h):
+        return piece(k, h, 0, WIDE // 2)
+
+    def high(k, h):
+        return piece(k, h, WIDE // 2, WIDE // 2)
 
     def g_tile(h):
         def loop_g(n, _):
             cols = pl.ds(pl.multiple_of(h * CHUNK + n * 512, 512), 512)
-            tile = dot(normg[...].reshape(1024, 256), cotg[:, :, cols].reshape(1024, 512), 0, 0)
-            gwf[:, :, cols] = tile.reshape(4, 64, 512)
-            gwt[:, :, cols] = tile.astype(BF16).reshape(4, 64, 512)
+            tile = dot(normg[...].reshape(256, 1024), cotg[:, :, cols].reshape(1024, 512), 1, 0)
+            gwf[:, :, cols] = tile.reshape(16, 16, 512)
+            gwt[:, :, cols] = tile.astype(BF16).reshape(16, 16, 512)
             return 0
 
         lax.fori_loop(0, CHUNK // 512, loop_g, 0)
 
     def g_first(h):
-        low, high = part(h, 0, CHUNK // 2), part(h, CHUNK // 2, CHUNK // 2)
-        begin(rcopy(gwt.at[two, :, low], xh_in.at[h, 0], xa_s.at[h, 0], xa_r.at[h, 0], x_up))
-        begin(rcopy(gwt.at[two, :, high], xh_in.at[h, 1], xa_s.at[h, 1], xa_r.at[h, 1], x_dn))
+        begin(rcopy(gwt.at[low(two, h)], xh_in.at[h, 0], xa_s.at[h, 0], xa_r.at[h, 0], x_up))
+        begin(rcopy(gwt.at[high(two, h)], xh_in.at[h, 1], xa_s.at[h, 1], xa_r.at[h, 1], x_dn))
 
     def g_second(h):
-        low, high = part(h, 0, CHUNK // 2), part(h, CHUNK // 2, CHUNK // 2)
-        lows, highs = pl.ds(0, CHUNK // 2), pl.ds(CHUNK // 2, CHUNK // 2)
         for a, to in ((0, x_up), (1, x_dn)):
             rcopy(xh_in.at[h, a], xh_in.at[h, a], xa_s.at[h, a], xa_r.at[h, a], to).wait_recv()
-        x_out[h, 0, :, lows] = (gwf[one_up, :, low] + xh_in[h, 0].astype(F32)).astype(BF16)
-        x_out[h, 0, :, highs] = gwt[one_up, :, high]
-        x_out[h, 1, :, lows] = gwt[one_dn, :, low]
-        x_out[h, 1, :, highs] = (gwf[one_dn, :, high] + xh_in[h, 1].astype(F32)).astype(BF16)
+        x_out[h, 0, :, :, lows] = (gwf[low(one_up, h)] + xh_in[h, 0].astype(F32)).astype(BF16)
+        x_out[h, 0, :, :, highs] = gwt[high(one_up, h)]
+        x_out[h, 1, :, :, lows] = gwt[low(one_dn, h)]
+        x_out[h, 1, :, :, highs] = (gwf[high(one_dn, h)] + xh_in[h, 1].astype(F32)).astype(BF16)
         begin(rcopy(x_out.at[h, 0], x_in.at[h, 0], xb_s.at[h, 0], xb_r.at[h, 0], x_up))
         begin(rcopy(x_out.at[h, 1], x_in.at[h, 1], xb_s.at[h, 1], xb_r.at[h, 1], x_dn))
 
     def g_third(h):
         for a, to in ((0, x_up), (1, x_dn)):
             rcopy(x_in.at[h, a], x_in.at[h, a], xb_s.at[h, a], xb_r.at[h, a], to).wait_recv()
-        total = gwf[x, :, part(h, 0, CHUNK)] + x_in[h, 0].astype(F32) + x_in[h, 1].astype(F32)
-        for zz in range(NZ):
-            z_out[h, zz] = total[:, zz * PIECE : (zz + 1) * PIECE].astype(BF16)
+        total = gwf[piece(x, h, 0, WIDE)] + x_in[h, 0].astype(F32) + x_in[h, 1].astype(F32)
+        z_out[h] = total.astype(BF16)
         for t in range(1, NZ):
             zz = (z + t) % NZ
             begin(rcopy(z_out.at[h, zz], z_in.at[h, z], z_s.at[h, zz], z_r.at[h, z], at_z(zz)))
         z_in[h, z] = z_out[h, z]
 
+    me_f = (2 * (y % 2) + c) * 2 + xh
+
     def f_copy(h, t):
-        return rcopy(f_out.at[h], f_in.at[h, z], f_s.at[h, t], f_r.at[h, z], final_to(t))
+        return rcopy(f_out.at[h], f_in.at[h, me_f], f_s.at[h, t], f_r.at[h, me_f], final_to(t))
 
     def g_fourth(h):
         for t in range(1, NZ):
@@ -416,18 +437,19 @@
 
             @pl.when(same(to))
             def _():
-                f_in[h, z] = f_out[h]
+                f_in[h, me_f] = f_out[h]
 
     def g_end(h):
-        for zz in range(NZ):
-            source = final_from(zz)
+        for t in range(8):
+            source = final_from(t)
 
             @pl.when(jnp.logical_not(same(source)))
-            def _(source=source, zz=zz):
-                ref = f_in.at[h, zz]
-                rcopy(ref, ref, f_s.at[h, zz], f_r.at[h, zz], source).wait_recv()
-
-            gw_ref[:, h * CHUNK + zz * PIECE : h * CHUNK + (zz + 1) * PIECE] = f_in[h, zz].astype(F32) * loss_scale
+            def _(source=source, t=t):
+                ref = f_in.at[h, t]
+                rcopy(ref, ref, f_s.at[h, t], f_r.at[h, t], source).wait_recv()
+
+            row, col = 16 * (t // 2), h * CHUNK + WIDE * (t % 2)
+            gw_ref[row : row + 16, col : col + WIDE] = f_in[h, t].astype(F32) * loss_scale
         for t in range(8):
             to = final_to(t)
 
@@ -459,7 +481,9 @@
         inv = lax.rsqrt(jnp.mean(a * a, axis=-1, keepdims=True) + EPSILON)
         att[:, cols] = a
         inverse[h] = inv
-        normed[:, cols] = (a * inv * gain_ref[:, cols]).astype(BF16)
+        out = a * inv * gain_ref[:, cols]
+        normed[:, cols] = out.astype(BF16)
+        flipped[h] = jnp.transpose(out).astype(BF16).reshape(8, 16, HEAD)
         return 0
 
     def loop_d(h, _):
@@ -502,47 +526,56 @@
     w_first()
     c_first()
     scan_spread(0)
-    lax.fori_loop(0, 16, loop_b, 0, unroll=2)
     wfull[i] = w_ref[...]
     cotg[cslot(0)] = cot_ref[...]
+    w_step(1)
+    lax.fori_loop(0, 16, loop_b, 0, unroll=2)
     scan_return(0)
-    w_step(1)
-    w_other(0)
+    w_step(2)
     c_second()
+    w_rest(1)
+    w_rest(7)
+    w_rest(2)
+    w_rest(6)
     scan_share(0, prefix)
+    w_step(3)
     scan_wait(0, prefix)
-    w_step(2)
     lax.fori_loop(0, 16, loop_n, 0, unroll=2)
     n_send()
-    w_other(7)
-    w_other(1)
     c_third()
-    w_step(3)
+    w_last()
+    for r in (0, 1, 7):
+        w_other(r)
+    for r in (3, 5):
+        w_rest(r)
+    for r in (2, 6):
+        w_other(r)
+    w_rest(4)
     c_wait()
+    for r in (3, 5, 4):
+        w_other(r)
+    w_pair_wait()
+    lax.fori_loop(0, 8, loop_c, 0)
     n_wait()
     for h in range(CHUNKS):
         g_tile(h)
         g_first(h)
-    w_other(6)
-    w_other(2)
-    w_last()
-    for h in range(CHUNKS):
-        g_second(h)
-    for r in (5, 3, 4):
-        w_other(r)
-    w_pair_wait()
-    lax.fori_loop(0, 8, loop_c, 0)
     lax.fori_loop(0, 16, loop_d, 0, unroll=2)
     scan_pair(1)
-    g_third(0)
+    g_second(0)
     scan_spread(1)
     for h in range(1, CHUNKS):
+        g_second(h)
+    lax.fori_loop(0, 8, loop_e, 0, unroll=2)
+    g_third(0)
+    lax.fori_loop(8, 16, loop_e, 0, unroll=2)
+    for h in range(1, CHUNKS):
         g_third(h)
-    lax.fori_loop(0, 16, loop_e, 0, unroll=2)
     scan_return(1)
-    for h in range(CHUNKS):
+    g_fourth(0)
+    lax.fori_loop(0, 4, loop_m, 0)
+    for h in range(1, CHUNKS):
         g_fourth(h)
-    lax.fori_loop(0, 4, loop_m, 0)
     scan_share(1, suffix)
     scan_wait(1, suffix)
     lax.fori_loop(0, 16, loop_f, 0, unroll=2)
@@ -572,9 +605,10 @@
         pltpu.VMEM((length, width), BF16),
         pltpu.VMEM((length, width), BF16),
         pltpu.VMEM((length, width), BF16),
+        pltpu.VMEM((1, width), F32),
         pltpu.VMEM((rows, width), BF16),
         pltpu.VMEM((length, width), BF16),
-        dma((5,)),
+        dma((6,)),
         pltpu.VMEM((length, width), BF16),
         pltpu.VMEM((length, width), BF16),
         pltpu.VMEM(states, BF16),
@@ -597,18 +631,19 @@
         pltpu.VMEM(states, BF16),
         pltpu.VMEM((32, 64, width), BF16),
         pltpu.VMEM((8, length, width), BF16),
-        pltpu.VMEM((8, length, 256), BF16),
-        pltpu.VMEM((4, 64, width), F32),
-        pltpu.VMEM((4, 64, width), BF16),
-        pltpu.VMEM((CHUNKS, 2, 64, CHUNK // 2), BF16),
-        pltpu.VMEM((CHUNKS, 2, 64, CHUNK), BF16),
-        pltpu.VMEM((CHUNKS, 2, 64, CHUNK), BF16),
-        pltpu.VMEM((CHUNKS, 8, 64, PIECE), BF16),
-        pltpu.VMEM((CHUNKS, 8, 64, PIECE), BF16),
-        pltpu.VMEM((CHUNKS, 64, PIECE), BF16),
-        pltpu.VMEM((CHUNKS, 8, 64, PIECE), BF16),
+        pltpu.VMEM((16, 8, 16, length), BF16),
+        pltpu.VMEM((16, 16, 8 * length), BF16),
+        pltpu.VMEM((16, 16, width), F32),
+        pltpu.VMEM((16, 16, width), BF16),
+        pltpu.VMEM((CHUNKS, 2, 8, 16, WIDE // 2), BF16),
+        pltpu.VMEM((CHUNKS, 2, 8, 16, WIDE), BF16),
+        pltpu.VMEM((CHUNKS, 2, 8, 16, WIDE), BF16),
+        pltpu.VMEM((CHUNKS, 8, 16, WIDE), BF16),
+        pltpu.VMEM((CHUNKS, 8, 16, WIDE), BF16),
+        pltpu.VMEM((CHUNKS, 16, WIDE), BF16),
+        pltpu.VMEM((CHUNKS, 8, 16, WIDE), BF16),
         dma((2,)), dma((2,)), dma((2, 16)), dma((2, 16)), dma((2, 16)), dma((2, 16)), dma((2,)), dma((2,)),
-        dma((4,)), dma((4,)), dma((4,)), dma((4,)), dma((8, 2)), dma((8, 2)), dma((16,)), dma((16,)),
+        dma((4,)), dma((4,)), dma((4,)), dma((4,)), dma((8, 2)), dma((8, 2)), dma((8, 2)), dma((8, 2)), dma((16,)), dma((16,)),
         dma((2,)), dma((2,)), dma((2,)), dma((2,)), dma((4,)), dma((4,)),
         dma((8,)), dma((8,)),
         dma((CHUNKS, 2)), dma((CHUNKS, 2)), dma((CHUNKS, 2)), dma((CHUNKS, 2)),
@@ -622,14 +657,18 @@
     results = pl.pallas_call(
         body,
         out_shape=shapes,
-        in_specs=[hbm, hbm, hbm, vmem, hbm, hbm],
+        in_specs=[hbm] * 6,
         out_specs=(vmem,) * 5,
         scratch_shapes=scratch,
         compiler_params=pltpu.CompilerParams(
             collective_id=0, has_side_effects=True, vmem_limit_bytes=44 * 1024 * 1024
         ),
         name="layer",
-    )(query_rows[0], key_rows[0], value_rows[0], norm_gain.reshape(1, width), out_weight, cotangent[0])
+    )(
+        *(pltpu.with_memory_space_constraint(a, pltpu.HBM) for a in (query_rows[0], key_rows[0], value_rows[0])),
+        pltpu.with_memory_space_constraint(norm_gain.reshape(1, width), pltpu.HBM),
+        *(pltpu.with_memory_space_constraint(a, pltpu.HBM) for a in (out_weight, cotangent[0])),
+    )
     anywhere = pl.BlockSpec(memory_space=pl.ANY)
     mixed, gq, gk, gv, gw = pl.pallas_call(
         finish,

time: 118 us -> 92.2 us (0.78)
  the two profiles are of different devices: /device:TPU:56 before, /device:TPU:1 now
where the time goes in v3:
time: 92.2 us; the launch traced here: 92.1 us
  Pallas kernels  91.5 us (99%)
    pallas_call x1, Pallas kernels, on_device(): pl.pallas_call(body, out_shape=shapes, in_specs=[hbm] * 6, out_specs=(vme...  90 us

profile of v3, /device:TPU:1, one launch (start us, length us, event | category | flops | bytes accessed | tf_op | source)
XLA Modules:
  0.0 92.1 jit_solution(5389253613187241252)
XLA Ops:
  0.6 90.0 %layer.1 = (bf16[128,2048]{1,0:T(8,128)(2,1)S(1)}, bf16[128,2048]{1,0:T(8,128)(2,1)S(1)}, bf16[128,2048]{1,0:T(8,128)(2,1)S(1)}, bf16[128,2048]{1,0:T(8,128)(2,1)S(1)}, f32[64,2048]{1,0:T(8,128)S(1)}) custom-call(bf16[128,2048]{1,0:T(8,128)(2,1)} %bitcast.9, bf16[128,2048]{1,0:T(8,128)(2,1)} %bitcast.10, bf16[128,2048]{1,0:T(8,128)(2,1)} %bitcast.11, ...), custom_call_target="tpu_custom_call" | custom-call | tf_op jit(solution)/shard_map/layer/pallas_call | solution.py:657
  90.6 1.5 %finish.1 = (bf16[128,2048]{1,0:T(8,128)(2,1)}, bf16[128,2048]{1,0:T(8,128)(2,1)}, bf16[128,2048]{1,0:T(8,128)(2,1)}, bf16[128,2048]{1,0:T(8,128)(2,1)}, f32[64,2048]{1,0:T(8,128)}) custom-call(bf16[128,2048]{1,0:T(8,128)(2,1)S(1)} %get-tuple-element.15.refs_0_, bf16[128,2048]{1,0:T(8,128)(2,1)S(1)} %get-tuple-element.16.refs_1_, ...), custom_call_target="tpu_custom_call" | custom-call | tf_op jit(solution)/shard_map/finish/pallas_call | solution.py:673

commit v4 on v3

--- a/solution.py
+++ b/solution.py
@@ -132,7 +132,7 @@
 
     for load in loads[:3]:
         load.wait()
-    lax.fori_loop(0, 16, loop_a, 0, unroll=2)
+    lax.fori_loop(0, 16, loop_a, 0, unroll=4)
     for load in loads[3:]:
         load.wait()
 
@@ -529,7 +529,7 @@
     wfull[i] = w_ref[...]
     cotg[cslot(0)] = cot_ref[...]
     w_step(1)
-    lax.fori_loop(0, 16, loop_b, 0, unroll=2)
+    lax.fori_loop(0, 16, loop_b, 0, unroll=4)
     scan_return(0)
     w_step(2)
     c_second()
@@ -540,7 +540,7 @@
     scan_share(0, prefix)
     w_step(3)
     scan_wait(0, prefix)
-    lax.fori_loop(0, 16, loop_n, 0, unroll=2)
+    lax.fori_loop(0, 16, loop_n, 0, unroll=4)
     n_send()
     c_third()
     w_last()
@@ -552,23 +552,23 @@
         w_other(r)
     w_rest(4)
     c_wait()
+    n_wait()
+    for h in range(CHUNKS):
+        g_tile(h)
+        g_first(h)
     for r in (3, 5, 4):
         w_other(r)
     w_pair_wait()
     lax.fori_loop(0, 8, loop_c, 0)
-    n_wait()
-    for h in range(CHUNKS):
-        g_tile(h)
-        g_first(h)
-    lax.fori_loop(0, 16, loop_d, 0, unroll=2)
+    lax.fori_loop(0, 16, loop_d, 0, unroll=4)
     scan_pair(1)
     g_second(0)
     scan_spread(1)
     for h in range(1, CHUNKS):
         g_second(h)
-    lax.fori_loop(0, 8, loop_e, 0, unroll=2)
+    lax.fori_loop(0, 8, loop_e, 0, unroll=4)
     g_third(0)
-    lax.fori_loop(8, 16, loop_e, 0, unroll=2)
+    lax.fori_loop(8, 16, loop_e, 0, unroll=4)
     for h in range(1, CHUNKS):
         g_third(h)
     scan_return(1)
@@ -578,7 +578,7 @@
         g_fourth(h)
     scan_share(1, suffix)
     scan_wait(1, suffix)
-    lax.fori_loop(0, 16, loop_f, 0, unroll=2)
+    lax.fori_loop(0, 16, loop_f, 0, unroll=4)
     for copy in pending:
         copy.wait_send()
     for h in range(CHUNKS):

time: 92.2 us -> 87.8 us (0.952)
  Pallas kernels: 91.5 us -> 87.1 us
    pallas_call x1, Pallas kernels: 90 us -> 85.6 us  [on_device(): pl.pallas_call(body, out_shape=shapes, in_specs=[hbm] * 6, out_specs=(vme...]
where the time goes in v4:
time: 87.8 us; the launch traced here: 87.7 us
  Pallas kernels  87.1 us (99%)
    pallas_call x1, Pallas kernels, on_device(): pl.pallas_call(body, out_shape=shapes, in_specs=[hbm] * 6, out_specs=(vme...  85.6 us

profile of v4, /device:TPU:1, one launch (start us, length us, event | category | flops | bytes accessed | tf_op | source)
XLA Modules:
  0.0 87.7 jit_solution(2537897405871959055)
XLA Ops:
  0.6 85.6 %layer.1 = (bf16[128,2048]{1,0:T(8,128)(2,1)S(1)}, bf16[128,2048]{1,0:T(8,128)(2,1)S(1)}, bf16[128,2048]{1,0:T(8,128)(2,1)S(1)}, bf16[128,2048]{1,0:T(8,128)(2,1)S(1)}, f32[64,2048]{1,0:T(8,128)S(1)}) custom-call(bf16[128,2048]{1,0:T(8,128)(2,1)} %bitcast.9, bf16[128,2048]{1,0:T(8,128)(2,1)} %bitcast.10, bf16[128,2048]{1,0:T(8,128)(2,1)} %bitcast.11, ...), custom_call_target="tpu_custom_call" | custom-call | tf_op jit(solution)/shard_map/layer/pallas_call | solution.py:657
  86.2 1.5 %finish.1 = (bf16[128,2048]{1,0:T(8,128)(2,1)}, bf16[128,2048]{1,0:T(8,128)(2,1)}, bf16[128,2048]{1,0:T(8,128)(2,1)}, bf16[128,2048]{1,0:T(8,128)(2,1)}, f32[64,2048]{1,0:T(8,128)}) custom-call(bf16[128,2048]{1,0:T(8,128)(2,1)S(1)} %get-tuple-element.15.refs_0_, bf16[128,2048]{1,0:T(8,128)(2,1)S(1)} %get-tuple-element.16.refs_1_, ...), custom_call_target="tpu_custom_call" | custom-call | tf_op jit(solution)/shard_map/finish/pallas_call | solution.py:673

commit v5 on v4

--- a/solution.py
+++ b/solution.py
@@ -132,7 +132,7 @@
 
     for load in loads[:3]:
         load.wait()
-    lax.fori_loop(0, 16, loop_a, 0, unroll=4)
+    lax.fori_loop(0, 16, loop_a, 0, unroll=8)
     for load in loads[3:]:
         load.wait()
 
@@ -247,8 +247,8 @@
             rcopy(ref, ref, wx_s.at[r, a], wx_r.at[r, a], near_x).wait_recv()
         begin(rcopy(wfull.at[slot], wfull.at[slot], wp_s.at[8 + r], wp_r.at[8 + r], partner))
 
-    def w_pair_wait():
-        for r in range(16):
+    def w_pair_wait(own):
+        for r in range(8) if own else range(8, 16):
             zz = (z + r) % NZ
             side = xl if r < 8 else 1 - xl
             ref = wfull.at[(side * NZ + zz) * 2 + o]
@@ -522,6 +522,12 @@
         gv_ref[:, cols] = (dgv[:, cols] + dot(fk[:, cols], s, 1, 0)).astype(BF16)
         return 0
 
+    def half(body, core):
+        lax.fori_loop(0, 8, lambda h, _: body(h + 8 * core, 0), 0, unroll=8)
+
+    def weights(side):
+        lax.fori_loop(0, 4, lambda h, _: loop_c(h + 4 * side, 0), 0, unroll=4)
+
     scan_pair(0)
     w_first()
     c_first()
@@ -529,7 +535,7 @@
     wfull[i] = w_ref[...]
     cotg[cslot(0)] = cot_ref[...]
     w_step(1)
-    lax.fori_loop(0, 16, loop_b, 0, unroll=4)
+    lax.fori_loop(0, 16, loop_b, 0, unroll=8)
     scan_return(0)
     w_step(2)
     c_second()
@@ -539,8 +545,9 @@
     w_rest(6)
     scan_share(0, prefix)
     w_step(3)
+    half(loop_n, c)
     scan_wait(0, prefix)
-    lax.fori_loop(0, 16, loop_n, 0, unroll=4)
+    half(loop_n, o)
     n_send()
     c_third()
     w_last()
@@ -558,17 +565,20 @@
         g_first(h)
     for r in (3, 5, 4):
         w_other(r)
-    w_pair_wait()
-    lax.fori_loop(0, 8, loop_c, 0)
-    lax.fori_loop(0, 16, loop_d, 0, unroll=4)
+    w_pair_wait(True)
+    weights(xl)
+    half(loop_d, xl)
+    w_pair_wait(False)
+    weights(1 - xl)
+    half(loop_d, 1 - xl)
     scan_pair(1)
     g_second(0)
     scan_spread(1)
     for h in range(1, CHUNKS):
         g_second(h)
-    lax.fori_loop(0, 8, loop_e, 0, unroll=4)
+    lax.fori_loop(0, 8, loop_e, 0, unroll=8)
     g_third(0)
-    lax.fori_loop(8, 16, loop_e, 0, unroll=4)
+    lax.fori_loop(8, 16, loop_e, 0, unroll=8)
     for h in range(1, CHUNKS):
         g_third(h)
     scan_return(1)
@@ -577,8 +587,9 @@
     for h in range(1, CHUNKS):
         g_fourth(h)
     scan_share(1, suffix)
+    half(loop_f, c)
     scan_wait(1, suffix)
-    lax.fori_loop(0, 16, loop_f, 0, unroll=4)
+    half(loop_f, o)
     for copy in pending:
         copy.wait_send()
     for h in range(CHUNKS):

time: 87.8 us -> 84.1 us (0.958)
  Pallas kernels: 87.1 us -> 83.4 us
    pallas_call x1, Pallas kernels: 85.6 us -> 81.9 us  [on_device(): pl.pallas_call(body, out_shape=shapes, in_specs=[hbm] * 6, out_specs=(vme...]
where the time goes in v5:
time: 84.1 us; the launch traced here: 84 us
  Pallas kernels  83.4 us (99%)
    pallas_call x1, Pallas kernels, on_device(): pl.pallas_call(body, out_shape=shapes, in_specs=[hbm] * 6, out_specs=(vme...  81.9 us

profile of v5, /device:TPU:1, one launch (start us, length us, event | category | flops | bytes accessed | tf_op | source)
XLA Modules:
  0.0 84.0 jit_solution(4689312465664209434)
XLA Ops:
  0.6 81.9 %layer.1 = (bf16[128,2048]{1,0:T(8,128)(2,1)S(1)}, bf16[128,2048]{1,0:T(8,128)(2,1)S(1)}, bf16[128,2048]{1,0:T(8,128)(2,1)S(1)}, bf16[128,2048]{1,0:T(8,128)(2,1)S(1)}, f32[64,2048]{1,0:T(8,128)S(1)}) custom-call(bf16[128,2048]{1,0:T(8,128)(2,1)} %bitcast.9, bf16[128,2048]{1,0:T(8,128)(2,1)} %bitcast.10, bf16[128,2048]{1,0:T(8,128)(2,1)} %bitcast.11, ...), custom_call_target="tpu_custom_call" | custom-call | tf_op jit(solution)/shard_map/layer/pallas_call | solution.py:668
  82.5 1.5 %finish.1 = (bf16[128,2048]{1,0:T(8,128)(2,1)}, bf16[128,2048]{1,0:T(8,128)(2,1)}, bf16[128,2048]{1,0:T(8,128)(2,1)}, bf16[128,2048]{1,0:T(8,128)(2,1)}, f32[64,2048]{1,0:T(8,128)}) custom-call(bf16[128,2048]{1,0:T(8,128)(2,1)S(1)} %get-tuple-element.15.refs_0_, bf16[128,2048]{1,0:T(8,128)(2,1)S(1)} %get-tuple-element.16.refs_1_, ...), custom_call_target="tpu_custom_call" | custom-call | tf_op jit(solution)/shard_map/finish/pallas_call | solution.py:684

commit v6 on v5

--- a/solution.py
+++ b/solution.py
@@ -342,25 +342,27 @@
     def positions(b):
         return pl.ds(pl.multiple_of(b * HEAD, HEAD), HEAD)
 
-    def n_send():
+    def n_send(core):
+        some = pl.ds(8 * core, 8)
         for t in range(1, 8):
             b = (me8 + t) % 8
             begin(
                 rcopy(
-                    flipped.at[:, b],
-                    normg.at[:, :, positions(me8)],
-                    n_s.at[b],
-                    n_r.at[me8],
+                    flipped.at[some, b],
+                    normg.at[some, :, positions(me8)],
+                    n_s.at[core, b],
+                    n_r.at[core, me8],
                     at_y(b // 2, b % 2),
                 )
             )
-        normg[:, :, positions(me8)] = flipped[:, me8]
+        normg[some, :, positions(me8)] = flipped[some, me8]
 
     def n_wait():
-        for t in range(1, 8):
-            b = (me8 + t) % 8
-            ref = normg.at[:, :, positions(b)]
-            rcopy(ref, ref, n_s.at[b], n_r.at[b], partner).wait_recv()
+        for core in (0, 1):
+            for t in range(1, 8):
+                b = (me8 + t) % 8
+                ref = normg.at[pl.ds(8 * core, 8), :, positions(b)]
+                rcopy(ref, ref, n_s.at[core, b], n_r.at[core, b], partner).wait_recv()
 
     x_up = at_x((x + 1) % NX)
     x_dn = at_x((x + 3) % NX)
@@ -546,9 +548,10 @@
     scan_share(0, prefix)
     w_step(3)
     half(loop_n, c)
+    n_send(c)
     scan_wait(0, prefix)
     half(loop_n, o)
-    n_send()
+    n_send(o)
     c_third()
     w_last()
     for r in (0, 1, 7):
@@ -656,7 +659,7 @@
         dma((2,)), dma((2,)), dma((2, 16)), dma((2, 16)), dma((2, 16)), dma((2, 16)), dma((2,)), dma((2,)),
         dma((4,)), dma((4,)), dma((4,)), dma((4,)), dma((8, 2)), dma((8, 2)), dma((8, 2)), dma((8, 2)), dma((16,)), dma((16,)),
         dma((2,)), dma((2,)), dma((2,)), dma((2,)), dma((4,)), dma((4,)),
-        dma((8,)), dma((8,)),
+        dma((2, 8)), dma((2, 8)),
         dma((CHUNKS, 2)), dma((CHUNKS, 2)), dma((CHUNKS, 2)), dma((CHUNKS, 2)),
         dma((CHUNKS, 8)), dma((CHUNKS, 8)), dma((CHUNKS, 8)), dma((CHUNKS, 8)),
     ]

time: 84.1 us -> 84.2 us (level)
  no operation moved by 1% of the time
where the time goes in v6:
time: 84.2 us; the launch traced here: 84 us
  Pallas kernels  83.4 us (99%)
    pallas_call x1, Pallas kernels, on_device(): pl.pallas_call(body, out_shape=shapes, in_specs=[hbm] * 6, out_specs=(vme...  81.9 us

profile of v6, /device:TPU:1, one launch (start us, length us, event | category | flops | bytes accessed | tf_op | source)
XLA Modules:
  0.0 84.0 jit_solution(7923657236162213069)
XLA Ops:
  0.6 81.9 %layer.1 = (bf16[128,2048]{1,0:T(8,128)(2,1)S(1)}, bf16[128,2048]{1,0:T(8,128)(2,1)S(1)}, bf16[128,2048]{1,0:T(8,128)(2,1)S(1)}, bf16[128,2048]{1,0:T(8,128)(2,1)S(1)}, f32[64,2048]{1,0:T(8,128)S(1)}) custom-call(bf16[128,2048]{1,0:T(8,128)(2,1)} %bitcast.9, bf16[128,2048]{1,0:T(8,128)(2,1)} %bitcast.10, bf16[128,2048]{1,0:T(8,128)(2,1)} %bitcast.11, ...), custom_call_target="tpu_custom_call" | custom-call | tf_op jit(solution)/shard_map/layer/pallas_call | solution.py:671
  82.5 1.5 %finish.1 = (bf16[128,2048]{1,0:T(8,128)(2,1)}, bf16[128,2048]{1,0:T(8,128)(2,1)}, bf16[128,2048]{1,0:T(8,128)(2,1)}, bf16[128,2048]{1,0:T(8,128)(2,1)}, f32[64,2048]{1,0:T(8,128)}) custom-call(bf16[128,2048]{1,0:T(8,128)(2,1)S(1)} %get-tuple-element.15.refs_0_, bf16[128,2048]{1,0:T(8,128)(2,1)S(1)} %get-tuple-element.16.refs_1_, ...), custom_call_target="tpu_custom_call" | custom-call | tf_op jit(solution)/shard_map/finish/pallas_call | solution.py:687

commit v7 on v5

--- a/solution.py
+++ b/solution.py
@@ -17,6 +17,8 @@
 NY = 4
 CHIPS = 16
 HALF = 1024
+CHIPS_FAR_FIRST = sorted(range(1, CHIPS), key=lambda t: abs(t % NZ - NZ // 2))
+Z_FAR_FIRST = sorted(range(1, NZ), key=lambda t: abs(t - NZ // 2))
 CHUNKS = 2
 CHUNK = 2048 // CHUNKS
 WIDE = CHUNK // 2
@@ -302,7 +304,7 @@
         rcopy(xrecv.at[n], xrecv.at[n], sx_s.at[n], sx_r.at[n], partner).wait_recv()
         total = (local[own_heads] + xrecv[n].astype(F32)).astype(BF16)
         pieces[n] = total.reshape(CHIPS, 64, HEAD)
-        for t in range(1, CHIPS):
+        for t in CHIPS_FAR_FIRST:
             jj = (j + t) % CHIPS
             begin(rcopy(pieces.at[n, jj], got.at[n, j], s1_s.at[n, jj], s1_r.at[n, j], chip(jj)))
         got[n, j] = pieces[n, j]
@@ -317,7 +319,7 @@
         for jj in order:
             back_out[n, jj] = total.astype(BF16)
             total = total + got[n, jj].astype(F32)
-        for t in range(1, CHIPS):
+        for t in CHIPS_FAR_FIRST:
             jj = (j + t) % CHIPS
             begin(rcopy(back_out.at[n, jj], back_in.at[n, j], s2_s.at[n, jj], s2_r.at[n, j], chip(jj)))
         back_in[n, j] = back_out[n, j]
@@ -409,7 +411,7 @@
             rcopy(x_in.at[h, a], x_in.at[h, a], xb_s.at[h, a], xb_r.at[h, a], to).wait_recv()
         total = gwf[piece(x, h, 0, WIDE)] + x_in[h, 0].astype(F32) + x_in[h, 1].astype(F32)
         z_out[h] = total.astype(BF16)
-        for t in range(1, NZ):
+        for t in Z_FAR_FIRST:
             zz = (z + t) % NZ
             begin(rcopy(z_out.at[h, zz], z_in.at[h, z], z_s.at[h, zz], z_r.at[h, z], at_z(zz)))
         z_in[h, z] = z_out[h, z]

time: 84.1 us -> 84 us (level)
  no operation moved by 1% of the time
where the time goes in v7:
time: 84 us; the launch traced here: 83.9 us
  Pallas kernels  83.3 us (99%)
    pallas_call x1, Pallas kernels, on_device(): pl.pallas_call(body, out_shape=shapes, in_specs=[hbm] * 6, out_specs=(vme...  81.8 us

profile of v7, /device:TPU:1, one launch (start us, length us, event | category | flops | bytes accessed | tf_op | source)
XLA Modules:
  0.0 83.9 jit_solution(2506214204288707387)
XLA Ops:
  0.6 81.8 %layer.1 = (bf16[128,2048]{1,0:T(8,128)(2,1)S(1)}, bf16[128,2048]{1,0:T(8,128)(2,1)S(1)}, bf16[128,2048]{1,0:T(8,128)(2,1)S(1)}, bf16[128,2048]{1,0:T(8,128)(2,1)S(1)}, f32[64,2048]{1,0:T(8,128)S(1)}) custom-call(bf16[128,2048]{1,0:T(8,128)(2,1)} %bitcast.9, bf16[128,2048]{1,0:T(8,128)(2,1)} %bitcast.10, bf16[128,2048]{1,0:T(8,128)(2,1)} %bitcast.11, ...), custom_call_target="tpu_custom_call" | custom-call | tf_op jit(solution)/shard_map/layer/pallas_call | solution.py:670
  82.4 1.5 %finish.1 = (bf16[128,2048]{1,0:T(8,128)(2,1)}, bf16[128,2048]{1,0:T(8,128)(2,1)}, bf16[128,2048]{1,0:T(8,128)(2,1)}, bf16[128,2048]{1,0:T(8,128)(2,1)}, f32[64,2048]{1,0:T(8,128)}) custom-call(bf16[128,2048]{1,0:T(8,128)(2,1)S(1)} %get-tuple-element.15.refs_0_, bf16[128,2048]{1,0:T(8,128)(2,1)S(1)} %get-tuple-element.16.refs_1_, ...), custom_call_target="tpu_custom_call" | custom-call | tf_op jit(solution)/shard_map/finish/pallas_call | solution.py:686
